TPU v7x, 512 devices: a whole 4x4x16 slice. The times are simulated.
512 devices in a mesh: rows: 64 (over z_lo, y, core), ang: 8 (over z_hi, x).
Axes of the slice: x: 4, y: 4, z: 16 (z_hi: 2, z_lo: 8; z = z_hi * 8 + z_lo), core: 2. Of those that a mesh axis runs over, the one named last changes fastest.
Arguments:
- measured: bfloat16 [8, 2048, 2, 2048], P('ang', 'rows'), may hold values from -6 to 6
- slices: bfloat16 [2, 2048, 2, 2048], P(None, 'rows', None, 'ang'), may hold values from -5 to 5
- kernel_taps: bfloat16 [2, 65], replicated, may hold values from -1.25 to 1.25
- angle_freq: float32 [128, 2], replicated, may hold values from -40 to 40
- chosen: int32 [8], P('ang'), may hold values from 0 to 127
Outputs:
- grad_near: float32 [2048, 2, 2048], P('rows', None, 'ang')
- grad_far: float32 [2048, 2, 2048], P('rows', None, 'ang')
Inputs may be any that keep to these rules, and one draw needn't show every extreme that they name: `chosen`: indices into the angle table; an index may repeat.
All inputs are finite; a program needn't handle non-finite values.
Results may differ from a plain program's by a relative error of at most 0.014.
Values may be sent and summed in bfloat16 or wider, within the bound.
A program may use at most 64 MiB of HBM per device.

v0:
```python
import math

import jax
import jax.numpy as jnp
from jax import lax
from jax.sharding import PartitionSpec as P


def toeplitz(row_taps, out_width):
    tap_count = row_taps.shape[0]
    window = out_width + tap_count - 1
    padded = jnp.concatenate([row_taps, jnp.zeros((out_width,), row_taps.dtype)])
    tiled = jnp.tile(padded, out_width)[: out_width * window]
    return tiled.reshape(out_width, window).T


def kernel_pair(kernel_taps, out_width):
    return jnp.concatenate(
        [toeplitz(kernel_taps[0], out_width), toeplitz(kernel_taps[1], out_width)], axis=1
    )


def adjoint_taps(kernel_taps):
    return jnp.stack([kernel_taps[0][::-1], -kernel_taps[1][::-1]])


def correlate_columns(field, kernel):
    window, doubled = kernel.shape
    tile_len = doubled // 2
    half_taps = (window - tile_len) // 2
    leading, comps, length = field.shape
    blocks = length // tile_len
    padded = jnp.pad(field, ((0, 0), (0, 0), (half_taps, tile_len - half_taps)))
    main_part = padded[:, :, :length].reshape(leading, comps, blocks, tile_len)
    tail_part = padded[:, :, tile_len : tile_len + length].reshape(
        leading, comps, blocks, tile_len
    )[..., : 2 * half_taps]
    windows = jnp.concatenate([main_part, tail_part], axis=3)
    product = jnp.einsum("rpnw,wk->rpnk", windows, kernel, preferred_element_type=jnp.float32)
    real_part = product[:, 0, :, :tile_len] - product[:, 1, :, tile_len:]
    imag_part = product[:, 0, :, tile_len:] + product[:, 1, :, :tile_len]
    return (
        jnp.stack([real_part, imag_part], axis=1)
        .reshape(leading, comps, length)
        .astype(jnp.bfloat16)
    )


def correlate_rows(field, kernel):
    window, doubled = kernel.shape
    tile_len = doubled // 2
    half_taps = (window - tile_len) // 2
    leading, comps, length = field.shape
    blocks = leading // tile_len
    padded = jnp.pad(field, ((half_taps, tile_len - half_taps), (0, 0), (0, 0)))
    main_part = padded[:leading].reshape(blocks, tile_len, comps, length)
    tail_part = padded[tile_len : tile_len + leading].reshape(blocks, tile_len, comps, length)[
        :, : 2 * half_taps
    ]
    windows = jnp.concatenate([main_part, tail_part], axis=1)
    product = jnp.einsum("nwpc,wk->nkpc", windows, kernel, preferred_element_type=jnp.float32)
    real_part = product[:, :tile_len, 0] - product[:, tile_len:, 1]
    imag_part = product[:, tile_len:, 0] + product[:, :tile_len, 1]
    return (
        jnp.stack([real_part, imag_part], axis=2)
        .reshape(leading, comps, length)
        .astype(jnp.bfloat16)
    )


def complex_times(left, right):
    left = left.astype(jnp.float32)
    right = right.astype(jnp.float32)
    real_part = left[:, 0] * right[:, 0] - left[:, 1] * right[:, 1]
    imag_part = left[:, 0] * right[:, 1] + left[:, 1] * right[:, 0]
    return jnp.stack([real_part, imag_part], axis=1)


def conjugate_times(left, right):
    left = left.astype(jnp.float32)
    right = right.astype(jnp.float32)
    real_part = left[:, 0] * right[:, 0] + left[:, 1] * right[:, 1]
    imag_part = left[:, 0] * right[:, 1] - left[:, 1] * right[:, 0]
    return jnp.stack([real_part, imag_part], axis=1)


def incident(freq, row_pos, col_pos, length):
    scale = 2.0 * math.pi / length
    phase = scale * (freq[0] * row_pos[:, None] + freq[1] * col_pos[None, :])
    return jnp.stack([jnp.cos(phase), jnp.sin(phase)], axis=1)


def local(measured, slices, kernel_taps, angle_freq, chosen):
    rows_dev = measured.shape[1]
    length = measured.shape[3]
    backward_taps = adjoint_taps(kernel_taps)
    forward_kernel = kernel_pair(kernel_taps, 128)
    adjoint_kernel = kernel_pair(backward_taps, 128)
    gathered = lax.all_gather(slices, "ang", axis=3, tiled=True)
    near_slab = gathered[0]
    far_slab = gathered[1]
    start = lax.axis_index("rows") * rows_dev
    row_pos = (start + jnp.arange(rows_dev, dtype=jnp.int32)).astype(jnp.float32)
    col_pos = jnp.arange(length).astype(jnp.float32)
    onehot = (chosen[:, None] == jnp.arange(angle_freq.shape[0], dtype=jnp.int32)[None, :]).astype(
        jnp.float32
    )
    freqs = jnp.dot(onehot, angle_freq, precision=lax.Precision.HIGHEST)

    def along_rows(field, kernel):
        columns = lax.all_to_all(field, "rows", split_axis=2, concat_axis=0, tiled=True)
        result = lax.all_to_all(
            correlate_rows(columns, kernel), "rows", split_axis=0, concat_axis=2, tiled=True
        )
        return result

    member = 0
    entering = incident(freqs[member], row_pos, col_pos, length)
    entry0 = complex_times(near_slab, entering).astype(jnp.bfloat16)
    inner = along_rows(correlate_columns(entry0, forward_kernel), forward_kernel)
    entry1 = complex_times(far_slab, inner).astype(jnp.bfloat16)
    exit_field = along_rows(correlate_columns(entry1, forward_kernel), forward_kernel)
    residue = (exit_field.astype(jnp.float32) - measured[member].astype(jnp.float32)).astype(
        jnp.bfloat16
    )
    back_far = correlate_columns(along_rows(residue, adjoint_kernel), adjoint_kernel)
    grad_far = conjugate_times(inner, back_far)
    carried_list = [conjugate_times(far_slab, back_far).astype(jnp.bfloat16)]
    member = 0
    entering = incident(freqs[member], row_pos, col_pos, length)
    back_near = correlate_columns(along_rows(carried_list[member], adjoint_kernel), adjoint_kernel)
    grad_near = conjugate_times(entering, back_near)
    near_total, far_total = (
        lax.psum_scatter(
            grad_near.astype(jnp.bfloat16), "ang", scatter_dimension=2, tiled=True
        ).astype(jnp.float32),
        lax.psum_scatter(
            grad_far.astype(jnp.bfloat16), "ang", scatter_dimension=2, tiled=True
        ).astype(jnp.float32),
    )
    return (near_total, far_total)


def solution(mesh):
    return jax.shard_map(
        local,
        mesh=mesh,
        in_specs=(P("ang", "rows", None, None), P(None, "rows", None, "ang"), P(), P(), P("ang")),
        out_specs=(P("rows", None, "ang"), P("rows", None, "ang")),
        check_vma=False,
    )
```

profile of v0, /device:TPU:1, one launch (start us, length us, event | category | flops | bytes accessed | tf_op | source)
XLA Modules:
  0.0 551.3 jit_solution(924524224001339390)
XLA Ops:
  10.1 64.8 %all_gather.3 = bf16[2,32,2,2048]{3,1,2,0:T(8,128)(2,1)S(1)} all-gather(bf16[2,32,2,256]{3,1,2,0:T(8,128)(2,1)S(1)} %copy.167), channel_id=1, replica_groups=mesh['rows'=64,'ang'=8] {'ang'}, dimensions={3}, use_global_device_ids=true | all-gather | bytes 589824 | tf_op jit(solution)/shard_map/all_gather | solution.py:99
  75.6 1.2 subtract_convert_fusion.4
  80.5 36.5 %all_to_all.126 = bf16[64,2,1024]{2,1,0:T(2,128)(2,1)S(1)} all-to-all(bf16[64,2,1024]{2,1,0:T(2,128)(2,1)S(1)} %reshape.301), channel_id=1, replica_groups=mesh['rows'=64,'ang'=8] {'rows'}, dimensions={0} | all-to-all | bytes 524288 | tf_op jit(solution)/shard_map/all_to_all | solution.py:111
  122.2 25.7 %all_to_all.127 = bf16[64,2,1024]{2,1,0:T(2,128)(2,1)S(1)} all-to-all(bf16[64,2,1024]{2,1,0:T(2,128)(2,1)S(1)} %reshape.303), channel_id=1, replica_groups=mesh['rows'=64,'ang'=8] {'rows'}, dimensions={0} | all-to-all | bytes 524288 | tf_op jit(solution)/shard_map/all_to_all | solution.py:112
  149.1 2.1 reshape.279
  151.1 3.2 copy.181
  158.0 25.6 %all_to_all.128 = bf16[64,2,1024]{2,1,0:T(2,128)(2,1)S(1)} all-to-all(bf16[64,2,1024]{2,1,0:T(2,128)(2,1)S(1)} %reshape.305), channel_id=1, replica_groups=mesh['rows'=64,'ang'=8] {'rows'}, dimensions={0} | all-to-all | bytes 524288 | tf_op jit(solution)/shard_map/all_to_all | solution.py:111
  188.7 25.8 %all_to_all.129 = bf16[64,2,1024]{2,1,0:T(2,128)(2,1)S(1)} all-to-all(bf16[64,2,1024]{2,1,0:T(2,128)(2,1)S(1)} %reshape.307), channel_id=1, replica_groups=mesh['rows'=64,'ang'=8] {'rows'}, dimensions={0} | all-to-all | bytes 524288 | tf_op jit(solution)/shard_map/all_to_all | solution.py:112
  215.6 2.1 reshape.280
  217.7 3.2 copy.193
  221.0 1.8 reshape.277
  222.7 1.2 fusion.9
  224.7 1.7 reshape.309
  226.4 5.9 %all-to-all-start.4 = ((bf16[64,2,1024]{2,1,0:T(2,128)(2,1)}), bf16[64,2,1024]{2,1,0:T(2,128)(2,1)S(1)}, u32[]{:S(2)}, u32[]{:S(2)}) async-start(bf16[64,2,1024]{2,1,0:T(2,128)(2,1)} %reshape.309), calls=%async_computation.4 | async-start | bytes 524288 | tf_op jit(solution)/shard_map/all_to_all | solution.py:111
  233.6 18.5 %all-to-all-done.4 = bf16[64,2,1024]{2,1,0:T(2,128)(2,1)S(1)} async-done(((bf16[64,2,1024]{2,1,0:T(2,128)(2,1)}), bf16[64,2,1024]{2,1,0:T(2,128)(2,1)S(1)}, u32[]{:S(2)}, u32[]{:S(2)}) %all-to-all-start.4) | async-done | bytes 262176 | tf_op jit(solution)/shard_map/all_to_all | solution.py:111
  257.2 26.0 %all_to_all.130 = bf16[64,2,1024]{2,1,0:T(2,128)(2,1)S(1)} all-to-all(bf16[64,2,1024]{2,1,0:T(2,128)(2,1)S(1)} %reshape.311), channel_id=1, replica_groups=mesh['rows'=64,'ang'=8] {'rows'}, dimensions={0} | all-to-all | bytes 524288 | tf_op jit(solution)/shard_map/all_to_all | solution.py:112
  288.4 25.6 %all_to_all.131 = bf16[64,2,1024]{2,1,0:T(2,128)(2,1)S(1)} all-to-all(bf16[64,2,1024]{2,1,0:T(2,128)(2,1)S(1)} %reshape.313), channel_id=1, replica_groups=mesh['rows'=64,'ang'=8] {'rows'}, dimensions={0} | all-to-all | bytes 524288 | tf_op jit(solution)/shard_map/all_to_all | solution.py:111
  318.0 1.7 reshape.315
  319.7 5.9 %all-to-all-start.7 = ((bf16[64,2,1024]{2,1,0:T(2,128)(2,1)}), bf16[64,2,1024]{2,1,0:T(2,128)(2,1)S(1)}, u32[]{:S(2)}, u32[]{:S(2)}) async-start(bf16[64,2,1024]{2,1,0:T(2,128)(2,1)} %reshape.315), calls=%async_computation.7 | async-start | bytes 524288 | tf_op jit(solution)/shard_map/all_to_all | solution.py:112
  326.7 18.8 %all-to-all-done.7 = bf16[64,2,1024]{2,1,0:T(2,128)(2,1)S(1)} async-done(((bf16[64,2,1024]{2,1,0:T(2,128)(2,1)}), bf16[64,2,1024]{2,1,0:T(2,128)(2,1)S(1)}, u32[]{:S(2)}, u32[]{:S(2)}) %all-to-all-start.7) | async-done | bytes 262176 | tf_op jit(solution)/shard_map/all_to_all | solution.py:112
  350.7 87.3 %reduce-scatter.5.cloned.1.call-done = bf16[32,2,256]{2,0,1:T(8,128)(2,1)} async-done(((bf16[32,2,2048]{2,0,1:T(8,128)(2,1)}), bf16[32,2,256]{2,0,1:T(8,128)(2,1)}) %reduce-scatter.5.cloned.1.call-update) | async-done | bytes 32784 | tf_op jit(solution)/shard_map/reduce_scatter | solution.py:137
  438.0 1.4 copy.220
  439.4 103.5 %reduce-scatter.3.cloned.1.call-done = bf16[32,2,256]{2,0,1:T(8,128)(2,1)} async-done(((bf16[32,2,2048]{2,0,1:T(8,128)(2,1)}), bf16[32,2,256]{2,0,1:T(8,128)(2,1)}) %reduce-scatter.3.cloned.1.call-update) | async-done | bytes 32784 | tf_op jit(solution)/shard_map/reduce_scatter | solution.py:134
  542.9 1.4 copy.219
  (162 shorter events, 44.7 us)
Async XLA Ops:
  7.2 0.7 copy-start
  74.9 2.1 copy-start.3
  220.9 1.8 copy-start.2
  226.4 25.8 %all-to-all-start.4 = ((bf16[64,2,1024]{2,1,0:T(2,128)(2,1)}), bf16[64,2,1024]{2,1,0:T(2,128)(2,1)S(1)}, u32[]{:S(2)}, u32[]{:S(2)}) async-start(bf16[64,2,1024]{2,1,0:T(2,128)(2,1)} %reshape.309), calls=%async_computation.4 | async-start | bytes 524288 | tf_op jit(solution)/shard_map/all_to_all | solution.py:111
  319.7 25.8 %all-to-all-start.7 = ((bf16[64,2,1024]{2,1,0:T(2,128)(2,1)}), bf16[64,2,1024]{2,1,0:T(2,128)(2,1)S(1)}, u32[]{:S(2)}, u32[]{:S(2)}) async-start(bf16[64,2,1024]{2,1,0:T(2,128)(2,1)} %reshape.315), calls=%async_computation.7 | async-start | bytes 524288 | tf_op jit(solution)/shard_map/all_to_all | solution.py:112
  325.7 112.3 %reduce-scatter.5.cloned.1.call-start = ((), (), s32[]{:S(2)}) async-start(), calls=%async_computation.11 | async-start | bytes 294912 | tf_op jit(solution)/shard_map/reduce_scatter | solution.py:137
  326.5 216.4 %reduce-scatter.3.cloned.1.call-start = ((), (), s32[]{:S(2)}) async-start(), calls=%async_computation.10 | async-start | bytes 294912 | tf_op jit(solution)/shard_map/reduce_scatter | solution.py:134
  348.2 196.1 %copy-start.1 = (f32[128,2]{0,1:T(2,128)S(1)}, f32[128,2]{0,1:T(2,128)}, u32[]{:S(2)}) copy-start(f32[128,2]{0,1:T(2,128)} %param.8) | copy-start | bytes 3076
Sparse Core Ops, SparseCore 0:
  330.9 106.9 reduce-scatter.4
  442.4 100.4 reduce-scatter.2
where the time goes:
time: 559 us; the launch traced here: 551 us
  blocking collectives  230 us (41%)
  waiting for transfers between devices  228 us (41%)
  local copies, waits for them, and re-layouts  54.7 us (10%)
  between operations  15.9 us (3%)
  starting transfers between devices  12.1 us (2%)
  other arithmetic  8.17 us (1%)
    reduce_scatter x1, waiting for transfers between devices, local(): lax.psum_scatter(grad_near.astype(jnp.bfloat16), 'ang', scatter_dimension...  103 us
    all_to_all x3, blocking collectives, along_rows(): lax.all_to_all(field, 'rows', split_axis=2, concat_axis=0, tiled=True)  87.6 us
    reduce_scatter x1, waiting for transfers between devices, local(): lax.psum_scatter(grad_far.astype(jnp.bfloat16), 'ang', scatter_dimension=...  87.3 us
    all_to_all x3, blocking collectives, along_rows(): lax.all_to_all(correlate_rows(columns, kernel), 'rows', split_axis=0, con...  77.4 us
    all_gather x1, blocking collectives, local(): gathered = lax.all_gather(slices, 'ang', axis=3, tiled=True)  64.8 us
    all_to_all x1, waiting for transfers between devices, along_rows(): lax.all_to_all(correlate_rows(columns, kernel), 'rows', split_axis=0, con...  18.8 us
    unnamed x47, local copies, waits for them, and re-layouts  18.7 us
    all_to_all x1, waiting for transfers between devices, along_rows(): lax.all_to_all(field, 'rows', split_axis=2, concat_axis=0, tiled=True)  18.5 us
  transfers between devices with their start and end apart: 4, of which 4 were waited for; matrix products, arithmetic and copies ran while one was open for 1% of the time, Pallas kernels for 0%

commit v1 on v0

v1 whole, which is shorter than its diff:
```python
import functools
import math

import jax
import jax.numpy as jnp
from jax import lax
from jax.experimental import pallas as pl
from jax.experimental.pallas import tpu as pltpu
from jax.sharding import PartitionSpec as P

MESH = pl.DeviceIdType.MESH
F32 = jnp.float32
BF16 = jnp.bfloat16
ROWS = 32
LANES = 128
UNITS = 9
REACH = 32
TAPS = 65


def build_taps(taps_ref, line, wf, wa, rf, ra):
    line[...] = jnp.zeros_like(line)
    line[0:2, 0:TAPS] = taps_ref[...].astype(F32)
    gr = line[0:1, :]
    gi = line[1:2, :]

    def column(vec, j):
        wide = jnp.broadcast_to(vec, (LANES, 4 * LANES))
        shift = (LANES * (j - 1) - REACH) % (4 * LANES)
        return pltpu.roll(wide, shift, 1, stride=1, stride_axis=0)[:, :LANES]

    for j in range(3):
        re = column(gr, j)
        im = column(gi, j)
        wa[j, 0:LANES, 0:LANES] = re.astype(BF16)
        wa[j, 0:LANES, LANES:] = (-im).astype(BF16)
        wa[j, LANES:, 0:LANES] = im.astype(BF16)
        wa[j, LANES:, LANES:] = re.astype(BF16)
        ret = re.T
        imt = im.T
        wf[2 - j, 0:LANES, 0:LANES] = ret.astype(BF16)
        wf[2 - j, 0:LANES, LANES:] = imt.astype(BF16)
        wf[2 - j, LANES:, 0:LANES] = (-imt).astype(BF16)
        wf[2 - j, LANES:, LANES:] = ret.astype(BF16)

    def row(vec, sign):
        narrow = vec[:, :LANES]
        ahead = pltpu.roll(jnp.broadcast_to(narrow, (ROWS, LANES)), 0, 1, stride=1, stride_axis=0)
        back = pltpu.roll(
            jnp.broadcast_to(narrow, (LANES, LANES)), LANES - 2 * REACH, 1, stride=1, stride_axis=0
        )
        return ahead, sign * back.T[0:ROWS, :]

    fr, br = row(gr, 1.0)
    fi, bi = row(gi, -1.0)
    rf[0:ROWS, :] = fr.astype(BF16)
    rf[ROWS:, :] = fi.astype(BF16)
    ra[0:ROWS, :] = br.astype(BF16)
    ra[ROWS:, :] = bi.astype(BF16)


def row_correlate(taps, window):
    both = jnp.dot(taps[:, 0 : 3 * ROWS], window, preferred_element_type=F32)
    re = both[:ROWS, :LANES] - both[ROWS:, LANES:]
    im = both[:ROWS, LANES:] + both[ROWS:, :LANES]
    return re, im


def times(ar, ai, br, bi):
    return ar * br - ai * bi, ar * bi + ai * br


def conj_times(ar, ai, br, bi):
    return ar * br + ai * bi, ar * bi - ai * br


def join(re, im):
    return jnp.concatenate([re, im], axis=-1)


def parts(value):
    value = value.astype(F32)
    return value[..., :LANES], value[..., LANES:]


def kernel(
    rows_n,
    length,
    chosen_ref,
    table_ref,
    taps_ref,
    near_ref,
    far_ref,
    meas_ref,
    out_near,
    out_far,
    near,
    far,
    other,
    freq,
    other_freq,
    line,
    wf,
    wa,
    rf,
    ra,
    inc,
    inner,
    field,
    halo,
    sum_near,
    sum_far,
    pack_near,
    pack_far,
    got_near,
    got_far,
    slab_send,
    slab_recv,
    edge_send,
    edge_recv,
    pair_send,
    pair_recv,
    halo_send,
    halo_recv,
    grad_send,
    grad_recv,
):
    r = lax.axis_index("rows")
    a = lax.axis_index("ang")
    zh = a // 4
    x = lax.rem(a, 4)
    has_up = r > 0
    has_dn = r < rows_n - 1
    up = lax.rem(r + rows_n - 1, rows_n)
    dn = lax.rem(r + 1, rows_n)
    pair = lax.rem(a + 4, 8)
    mine = zh + 2 * x

    barrier = pltpu.get_barrier_semaphore()
    for k in range(1, 8):
        pl.semaphore_signal(barrier, inc=1, device_id=(r, lax.rem(a + k, 8)), device_id_type=MESH)

    @pl.when(has_up)
    def _():
        pl.semaphore_signal(barrier, inc=1, device_id=(up, a), device_id_type=MESH)

    @pl.when(has_dn)
    def _():
        pl.semaphore_signal(barrier, inc=1, device_id=(dn, a), device_id_type=MESH)

    build_taps(taps_ref, line, wf, wa, rf, ra)
    fy = table_ref[chosen_ref[0], 0]
    fx = table_ref[chosen_ref[0], 1]
    row_id = lax.broadcasted_iota(jnp.int32, (8, LANES), 0)
    freq[...] = jnp.where(row_id < 4, jnp.full((8, LANES), fy, F32), jnp.full((8, LANES), fx, F32))

    base = 7 * zh

    def waves(t, ref):
        vy = ref[0:1, :]
        vx = ref[4:5, :]
        pos_r = (r * ROWS + lax.broadcasted_iota(jnp.int32, (ROWS, LANES), 0)).astype(F32)
        pos_c = (
            (base + lax.broadcasted_iota(jnp.int32, (16, LANES), 0)) * LANES
            + lax.broadcasted_iota(jnp.int32, (16, LANES), 1)
        ).astype(F32)
        turn_r = (vy * pos_r) * (1.0 / length)
        turn_c = (vx * pos_c) * (1.0 / length)
        ang_r = (2.0 * math.pi) * (turn_r - jnp.floor(turn_r + 0.5))
        ang_c = (2.0 * math.pi) * (turn_c - jnp.floor(turn_c + 0.5))
        cr, sr = jnp.cos(ang_r), jnp.sin(ang_r)
        cc, sc = jnp.cos(ang_c), jnp.sin(ang_c)
        for u in range(UNITS):
            re, im = times(cr, sr, cc[u : u + 1, :], sc[u : u + 1, :])
            inc[t, u, :, 0:LANES] = re
            inc[t, u, :, LANES:] = im

    waves(0, freq)
    for t in range(2):
        field[t, 0] = jnp.zeros((ROWS, 2 * LANES), BF16)
        field[t, UNITS + 1] = jnp.zeros((ROWS, 2 * LANES), BF16)

    @pl.when(jnp.logical_not(has_up))
    def _():
        halo[:, :, :, 0:ROWS, :] = jnp.zeros((4, 2, UNITS, ROWS, 2 * LANES), BF16)

    @pl.when(jnp.logical_not(has_dn))
    def _():
        halo[:, :, :, 2 * ROWS :, :] = jnp.zeros((4, 2, UNITS, ROWS, 2 * LANES), BF16)

    near[pl.ds(mine, 2)] = near_ref[...]
    far[pl.ds(mine, 2)] = far_ref[...]

    pl.semaphore_wait(barrier, 7 + has_up.astype(jnp.int32) + has_dn.astype(jnp.int32))

    slabs = ((near_ref, near), (far_ref, far))

    def slab_copy(i, k):
        src, dst = slabs[i]
        return pltpu.make_async_remote_copy(
            src_ref=src,
            dst_ref=dst.at[pl.ds(mine, 2)],
            send_sem=slab_send.at[i, k - 1],
            recv_sem=slab_recv.at[i, k - 1],
            device_id=(r, 4 * zh + lax.rem(x + k, 4)),
            device_id_type=MESH,
        )

    def edge_copy(i, k):
        src, dst = slabs[i]
        return pltpu.make_async_remote_copy(
            src_ref=src.at[pl.ds(1 - zh, 1)],
            dst_ref=dst.at[pl.ds(8 * zh, 1)],
            send_sem=edge_send.at[i, k],
            recv_sem=edge_recv.at[i],
            device_id=(r, 4 * (1 - zh) + k),
            device_id_type=MESH,
        )

    def edge_wait(i):
        src, dst = slabs[i]
        pltpu.make_async_remote_copy(
            src_ref=src.at[pl.ds(0, 1)],
            dst_ref=dst.at[pl.ds(8 * (1 - zh), 1)],
            send_sem=edge_send.at[i, 0],
            recv_sem=edge_recv.at[i],
            device_id=(r, pair),
            device_id_type=MESH,
        ).wait_recv()

    def slab_wait(i):
        for k in range(1, 4):
            slab_copy(i, k).wait_recv()

    freq_copy = pltpu.make_async_remote_copy(
        src_ref=freq,
        dst_ref=other_freq,
        send_sem=pair_send.at[0],
        recv_sem=pair_recv.at[0],
        device_id=(r, pair),
        device_id_type=MESH,
    )
    meas_copy = pltpu.make_async_remote_copy(
        src_ref=meas_ref.at[pl.ds(7 * (1 - zh), UNITS)],
        dst_ref=other,
        send_sem=pair_send.at[1],
        recv_sem=pair_recv.at[1],
        device_id=(r, pair),
        device_id_type=MESH,
    )
    owner = x == 3 * (1 - zh)

    @pl.when(owner)
    def _():
        for k in range(4):
            edge_copy(0, k).start()

    freq_copy.start()
    for k in range(1, 4):
        slab_copy(0, k).start()

    @pl.when(owner)
    def _():
        for k in range(4):
            edge_copy(1, k).start()

    for k in range(1, 4):
        slab_copy(1, k).start()
    meas_copy.start()

    def halo_copy(s, t, down):
        lo = 0 if down else 2 * ROWS
        i = 0 if down else 1
        return pltpu.make_async_remote_copy(
            src_ref=halo.at[s, t, :, ROWS : 2 * ROWS, :],
            dst_ref=halo.at[s, t, :, lo : lo + ROWS, :],
            send_sem=halo_send.at[s, t, i],
            recv_sem=halo_recv.at[s, t, i],
            device_id=(dn if down else up, a),
            device_id_type=MESH,
        )

    def halo_start(s, t):
        @pl.when(has_dn)
        def _():
            halo_copy(s, t, True).start()

        @pl.when(has_up)
        def _():
            halo_copy(s, t, False).start()

    def halo_wait(s, t):
        @pl.when(has_up)
        def _():
            halo_copy(s, t, True).wait_recv()

        @pl.when(has_dn)
        def _():
            halo_copy(s, t, False).wait_recv()

    def halo_done(s, t):
        @pl.when(has_dn)
        def _():
            halo_copy(s, t, True).wait_send()

        @pl.when(has_up)
        def _():
            halo_copy(s, t, False).wait_send()

    def each_unit(body):
        def step(u, carry):
            body(u)
            return carry

        lax.fori_loop(0, UNITS, step, 0, unroll=3)

    def columns(t, w, body):
        def step(c, carry):
            acc = None
            for j in range(3):
                lhs = field[t, pl.ds(3 * c + j, 3)].reshape(3 * ROWS, 2 * LANES)
                term = jnp.dot(lhs, w[j], preferred_element_type=F32)
                acc = term if acc is None else acc + term
            body(3 * c, acc.astype(BF16).reshape(3, ROWS, 2 * LANES))
            return carry

        lax.fori_loop(0, 3, step, 0)

    def own(s, t, u, value):
        halo[s, t, pl.ds(u, 3), ROWS : 2 * ROWS, :] = value

    def enter(t):
        def body(u):
            re, im = times(*parts(near[u]), *parts(inc[t, u]))
            field[t, u + 1] = join(re, im).astype(BF16)

        each_unit(body)
        columns(t, wf, lambda u, value: own(0, t, u, value))
        halo_start(0, t)

    def second(t):
        halo_wait(0, t)

        def body(u):
            re, im = row_correlate(rf, halo[0, t, u])
            value = join(re, im).astype(BF16)
            inner[t, u] = value
            re, im = times(*parts(far[u]), *parts(value))
            field[t, u + 1] = join(re, im).astype(BF16)

        each_unit(body)
        columns(t, wf, lambda u, value: own(1, t, u, value))
        halo_start(1, t)

    def compare(t, target):
        halo_wait(1, t)

        def body(u):
            re, im = row_correlate(rf, halo[1, t, u])
            value = join(re, im).astype(BF16)
            diff = value.astype(F32) - target(u).astype(F32)
            halo[2, t, u, ROWS : 2 * ROWS, :] = diff.astype(BF16)

        each_unit(body)
        halo_start(2, t)

    def back(s, t):
        halo_wait(s, t)

        def body(u):
            re, im = row_correlate(ra, halo[s, t, u])
            field[t, u + 1] = join(re, im).astype(BF16)

        each_unit(body)

    def back_far(t):
        back(2, t)

        def body(u, value):
            br, bi = parts(value)
            gr, gi = conj_times(*parts(inner[t, pl.ds(u, 3)]), br, bi)
            grad = join(gr, gi)
            if t == 0:
                sum_far[pl.ds(u, 3)] = grad
            else:
                grad = grad + sum_far[pl.ds(u, 3)]
                sum_far[pl.ds(u, 3)] = grad
                pack_far[pl.ds(u, 3)] = grad.astype(BF16)
            re, im = conj_times(*parts(far[pl.ds(u, 3)]), br, bi)
            own(3, t, u, join(re, im).astype(BF16))

        columns(t, wa, body)
        halo_start(3, t)

    def back_near(t):
        back(3, t)

        def body(u, value):
            gr, gi = conj_times(*parts(inc[t, pl.ds(u, 3)]), *parts(value))
            grad = join(gr, gi)
            if t == 0:
                sum_near[pl.ds(u, 3)] = grad
            else:
                grad = grad + sum_near[pl.ds(u, 3)]
                sum_near[pl.ds(u, 3)] = grad
                pack_near[pl.ds(u, 3)] = grad.astype(BF16)

        columns(t, wa, body)

    grads = ((pack_near, got_near), (pack_far, got_far))

    def grad_copy(i, k):
        src, dst = grads[i]
        to = lax.rem(x + k, 4)
        return pltpu.make_async_remote_copy(
            src_ref=src.at[pl.ds(zh + 2 * to, 2)],
            dst_ref=dst.at[k - 1],
            send_sem=grad_send.at[i, k - 1],
            recv_sem=grad_recv.at[i, k - 1],
            device_id=(r, 4 * zh + to),
            device_id_type=MESH,
        )

    slab_wait(0)
    edge_wait(0)
    enter(0)
    freq_copy.wait_recv()
    waves(1, other_freq)
    enter(1)
    slab_wait(1)
    edge_wait(1)
    second(0)
    second(1)
    compare(0, lambda u: meas_ref[7 * zh + u])
    meas_copy.wait_recv()
    compare(1, lambda u: other[u])
    back_far(0)
    back_far(1)
    for k in range(1, 4):
        grad_copy(1, k).start()
    back_near(0)
    back_near(1)
    for k in range(1, 4):
        grad_copy(0, k).start()

    def finish(i, total, got, out):
        for k in range(1, 4):
            grad_copy(i, k).wait_recv()
        value = total[pl.ds(mine, 2)]
        for k in range(3):
            value = value + got[k].astype(F32)
        out[...] = value

    finish(1, sum_far, got_far, out_far)
    finish(0, sum_near, got_near, out_near)

    for i in range(2):
        for k in range(1, 4):
            slab_copy(i, k).wait_send()
            grad_copy(i, k).wait_send()

        @pl.when(owner)
        def _():
            for k in range(4):
                edge_copy(i, k).wait_send()

    freq_copy.wait_send()
    meas_copy.wait_send()
    for s in range(4):
        for t in range(2):
            halo_done(s, t)


def local(rows_n, measured, slices, kernel_taps, angle_freq, chosen):
    length = measured.shape[3]
    blocks = length // LANES
    meas = measured[0].reshape(ROWS, 2, blocks, LANES).transpose(2, 0, 1, 3)
    meas = meas.reshape(blocks, ROWS, 2 * LANES)
    slabs = slices.reshape(2, ROWS, 2, 2, LANES).transpose(0, 3, 1, 2, 4)
    slabs = slabs.reshape(2, 2, ROWS, 2 * LANES)
    unit = (ROWS, 2 * LANES)
    vmem = pl.BlockSpec(memory_space=pltpu.VMEM)
    smem = pl.BlockSpec(memory_space=pltpu.SMEM)
    dma = pltpu.SemaphoreType.DMA
    out = jax.ShapeDtypeStruct((2,) + unit, F32)
    grad_near, grad_far = pl.pallas_call(
        functools.partial(kernel, rows_n, length),
        out_shape=(out, out),
        in_specs=[smem, smem, vmem, vmem, vmem, vmem],
        out_specs=(vmem, vmem),
        scratch_shapes=[
            pltpu.VMEM((UNITS,) + unit, BF16),
            pltpu.VMEM((UNITS,) + unit, BF16),
            pltpu.VMEM((UNITS,) + unit, BF16),
            pltpu.VMEM((8, LANES), F32),
            pltpu.VMEM((8, LANES), F32),
            pltpu.VMEM((8, 4 * LANES), F32),
            pltpu.VMEM((3, 2 * LANES, 2 * LANES), BF16),
            pltpu.VMEM((3, 2 * LANES, 2 * LANES), BF16),
            pltpu.VMEM((2 * ROWS, LANES), BF16),
            pltpu.VMEM((2 * ROWS, LANES), BF16),
            pltpu.VMEM((2, UNITS) + unit, F32),
            pltpu.VMEM((2, UNITS) + unit, BF16),
            pltpu.VMEM((2, UNITS + 2) + unit, BF16),
            pltpu.VMEM((4, 2, UNITS, 3 * ROWS, 2 * LANES), BF16),
            pltpu.VMEM((UNITS,) + unit, F32),
            pltpu.VMEM((UNITS,) + unit, F32),
            pltpu.VMEM((UNITS,) + unit, BF16),
            pltpu.VMEM((UNITS,) + unit, BF16),
            pltpu.VMEM((3, 2) + unit, BF16),
            pltpu.VMEM((3, 2) + unit, BF16),
            dma((2, 3)),
            dma((2, 3)),
            dma((2, 4)),
            dma((2,)),
            dma((2,)),
            dma((2,)),
            dma((4, 2, 2)),
            dma((4, 2, 2)),
            dma((2, 3)),
            dma((2, 3)),
        ],
        compiler_params=pltpu.CompilerParams(collective_id=0, has_side_effects=True),
    )(chosen, angle_freq, kernel_taps, slabs[0], slabs[1], meas)

    def place(grad):
        return grad.reshape(2, ROWS, 2, LANES).transpose(1, 2, 0, 3).reshape(ROWS, 2, 2 * LANES)

    return place(grad_near), place(grad_far)


def solution(mesh):
    return jax.shard_map(
        functools.partial(local, mesh.shape["rows"]),
        mesh=mesh,
        in_specs=(P("ang", "rows", None, None), P(None, "rows", None, "ang"), P(), P(), P("ang")),
        out_specs=(P("rows", None, "ang"), P("rows", None, "ang")),
        check_vma=False,
    )
```

time: 559 us -> 78.4 us (0.14)
  the two profiles are of different devices: /device:TPU:1 before, /device:TPU:32 now
where the time goes in v1:
time: 78.4 us; the launch traced here: 78.2 us
  Pallas kernels  71 us (91%)
  local copies, waits for them, and re-layouts  5.87 us (7%)
  between operations  1.37 us (2%)
    pallas_call x1, Pallas kernels, local(): pl.pallas_call(functools.partial(kernel, rows_n, length), out_shape=(out,...  71 us
    reshape x3, local copies, waits for them, and re-layouts, place(): grad.reshape(2, ROWS, 2, LANES).transpose(1, 2, 0, 3)  1.64 us
    unnamed x9, local copies, waits for them, and re-layouts  1.58 us

profile of v1, /device:TPU:32, one launch (start us, length us, event | category | flops | bytes accessed | tf_op | source)
XLA Modules:
  0.0 78.2 jit_solution(1114640190474417266)
XLA Ops:
  0.6 0.0 copy-start
  0.6 0.0 copy-start.1
  0.7 0.8 %copy-done = bf16[2,32,2,256]{3,2,1,0:T(2,128)(2,1)S(1)} copy-done((bf16[2,32,2,256]{3,2,1,0:T(2,128)(2,1)S(1)}, bf16[2,32,2,256]{3,2,1,0:T(2,128)(2,1)}, u32[]{:S(2)}) %copy-start) | copy-done | bytes 65560
  1.6 0.6 squeeze.6.near_ref
  2.2 0.6 squeeze.7.far_ref
  2.9 0.0 copy-done.1
  2.9 0.2 reshape_squeeze.3
  3.0 0.2 copy.19
  3.3 0.0 copy-start.3
  3.3 0.9 %reshape.28.meas_ref = bf16[16,32,256]{2,1,0:T(8,128)(2,1)} reshape(bf16[16,32,2,128]{3,2,1,0:T(2,128)(2,1)S(1)} %bitcast.22) | data formatting | bytes 524288 | tf_op jit(solution)/shard_map/reshape | solution.py:478
  4.2 0.0 copy-done.3
  4.2 0.7 copy.9.table_ref
  5.6 71.0 %shard_map.68 = (f32[2,32,256]{2,1,0:T(8,128)}, f32[2,32,256]{2,1,0:T(8,128)}) custom-call(s32[1]{0:T(128)S(6)} %copy.20.chosen_ref, f32[128,2]{1,0:T(8,128)} %copy.9.table_ref, bf16[2,65]{1,0:T(2,128)(2,1)} %taps_ref.1, bf16[2,32,256]{2,1,0:T(8,128)(2,1)} %squeeze.6.near_ref, bf16[2,32,256]{2,1,0:T(8,128)(2,1)} %squeeze.7.far_ref, ...), custom_call_target="tpu_custom_call" | custom-call | tf_op jit(solution)/shard_map/pallas_call | solution.py:486
  76.5 0.0 copy-start.2
  76.5 0.9 %reshape.29 = f32[2,32,2,128]{3,2,1,0:T(2,128)S(1)} reshape(f32[2,32,256]{2,1,0:T(8,128)} %get-tuple-element.4) | data formatting | bytes 131072 | tf_op jit(solution)/shard_map/reshape | solution.py:527
  77.4 0.0 copy-done.2
  77.5 0.7 copy_bitcast_fusion.1
  (3 shorter events, 0.1 us)
Async XLA Ops:
  0.6 0.8 %copy-start = (bf16[2,32,2,256]{3,2,1,0:T(2,128)(2,1)S(1)}, bf16[2,32,2,256]{3,2,1,0:T(2,128)(2,1)}, u32[]{:S(2)}) copy-start(bf16[2,32,2,256]{3,2,1,0:T(2,128)(2,1)} %param.6) | copy-start | bytes 196612
  0.6 2.2 %copy-start.1 = (bf16[1,32,2,2048]{3,2,1,0:T(2,128)(2,1)S(1)}, bf16[1,32,2,2048]{3,2,1,0:T(2,128)(2,1)}, u32[]{:S(2)}) copy-start(bf16[1,32,2,2048]{3,2,1,0:T(2,128)(2,1)} %param.5) | copy-start | bytes 786436
  3.3 0.9 %copy-start.3 = (f32[128,2]{0,1:T(2,128)S(1)}, f32[128,2]{0,1:T(2,128)}, u32[]{:S(2)}) copy-start(f32[128,2]{0,1:T(2,128)} %param.8) | copy-start | bytes 3076
  76.5 0.9 %copy-start.2 = (f32[2,32,256]{2,1,0:T(8,128)S(1)}, f32[2,32,256]{2,1,0:T(8,128)}, u32[]{:S(2)}) copy-start(f32[2,32,256]{2,1,0:T(8,128)} %get-tuple-element.5) | copy-start | bytes 196612

commit v2 on v1

v2 whole, which is shorter than its diff:
```python
import functools
import math

import jax
import jax.numpy as jnp
from jax import lax
from jax.experimental import pallas as pl
from jax.experimental.pallas import tpu as pltpu
from jax.sharding import PartitionSpec as P

MESH = pl.DeviceIdType.MESH
F32 = jnp.float32
BF16 = jnp.bfloat16
ROWS = 32
LANES = 128
UNITS = 9
REACH = 32
TAPS = 65


def build_taps(zh, taps_ref, line, wf, wa, rf, ra):
    line[...] = jnp.zeros_like(line)
    line[0:2, 0:TAPS] = taps_ref[...].astype(F32)
    gr = line[0:1, :]
    gi = line[1:2, :]

    def column(vec, j):
        wide = jnp.broadcast_to(vec, (LANES, 4 * LANES))
        shift = (LANES * (j - 1) - REACH) % (4 * LANES)
        return pltpu.roll(wide, shift, 1, stride=1, stride_axis=0)[:, :LANES]

    for j in range(3):
        re = column(gr, j)
        im = column(gi, j)
        ja = j + zh * (2 - 2 * j)
        jf = 2 - ja
        wa[ja, 0:LANES, 0:LANES] = re.astype(BF16)
        wa[ja, 0:LANES, LANES:] = (-im).astype(BF16)
        wa[ja, LANES:, 0:LANES] = im.astype(BF16)
        wa[ja, LANES:, LANES:] = re.astype(BF16)
        ret = re.T
        imt = im.T
        wf[jf, 0:LANES, 0:LANES] = ret.astype(BF16)
        wf[jf, 0:LANES, LANES:] = imt.astype(BF16)
        wf[jf, LANES:, 0:LANES] = (-imt).astype(BF16)
        wf[jf, LANES:, LANES:] = ret.astype(BF16)

    def row(vec, sign):
        narrow = vec[:, :LANES]
        ahead = pltpu.roll(jnp.broadcast_to(narrow, (ROWS, LANES)), 0, 1, stride=1, stride_axis=0)
        back = pltpu.roll(
            jnp.broadcast_to(narrow, (LANES, LANES)), LANES - 2 * REACH, 1, stride=1, stride_axis=0
        )
        return ahead, sign * back.T[0:ROWS, :]

    fr, br = row(gr, 1.0)
    fi, bi = row(gi, -1.0)
    rf[0:ROWS, :] = fr.astype(BF16)
    rf[ROWS:, :] = fi.astype(BF16)
    ra[0:ROWS, :] = br.astype(BF16)
    ra[ROWS:, :] = bi.astype(BF16)


def row_correlate(taps, window):
    both = jnp.dot(taps[:, 0 : 3 * ROWS], window, preferred_element_type=F32)
    re = both[:ROWS, :LANES] - both[ROWS:, LANES:]
    im = both[:ROWS, LANES:] + both[ROWS:, :LANES]
    return re, im


def times(ar, ai, br, bi):
    return ar * br - ai * bi, ar * bi + ai * br


def conj_times(ar, ai, br, bi):
    return ar * br + ai * bi, ar * bi - ai * br


def join(re, im):
    return jnp.concatenate([re, im], axis=-1)


def parts(value):
    value = value.astype(F32)
    return value[..., :LANES], value[..., LANES:]


PARTS = (((0, 7), (7, 9)), ((0, 6), (6, 9)), ((0, 3), (3, 6), (6, 9)), ((0, 3), (3, 6), (6, 9)))
PIECE = 3 * LANES


def kernel(
    rows_n,
    length,
    chosen_ref,
    table_ref,
    taps_ref,
    slices_ref,
    meas_ref,
    out_near,
    out_far,
    slab_raw,
    slab_wide,
    meas_raw,
    meas_wide,
    near,
    far,
    freq,
    other_freq,
    line,
    wf,
    wa,
    rf,
    ra,
    inc,
    inner,
    field,
    halo,
    sum_near,
    sum_far,
    pack_near,
    pack_far,
    got_near,
    got_far,
    load_sem,
    slab_send,
    slab_recv,
    edge_send,
    edge_recv,
    relay_send,
    relay_recv,
    freq_send,
    freq_recv,
    meas_send,
    meas_recv,
    halo_send,
    halo_recv,
    grad_send,
    grad_recv,
):
    r = lax.axis_index("rows")
    a = lax.axis_index("ang")
    zh = a // 4
    x = lax.rem(a, 4)
    has_up = r > 0
    has_dn = r < rows_n - 1
    up = lax.rem(r + rows_n - 1, rows_n)
    dn = lax.rem(r + 1, rows_n)
    pair = lax.rem(a + 4, 8)

    def first_of(other_x):
        return 2 * other_x + zh * (6 - 4 * other_x)

    mine = first_of(x)

    def flip(i, n):
        return i + zh * (n - 1 - 2 * i)

    barrier = pltpu.get_barrier_semaphore()
    pl.semaphore_signal(barrier, inc=1, device_id=(r, pair), device_id_type=MESH)
    for k in range(1, 4):
        to = (r, 4 * zh + lax.rem(x + k, 4))
        pl.semaphore_signal(barrier, inc=1, device_id=to, device_id_type=MESH)

    @pl.when(has_up)
    def _():
        pl.semaphore_signal(barrier, inc=1, device_id=(up, a), device_id_type=MESH)

    @pl.when(has_dn)
    def _():
        pl.semaphore_signal(barrier, inc=1, device_id=(dn, a), device_id_type=MESH)

    def piece_of(half, c):
        first = 7 * half + 3 * c + half * (6 - 6 * c)
        return meas_ref.at[0, :, :, pl.ds(pl.multiple_of(first * LANES, LANES), PIECE)]

    slab_load = pltpu.make_async_copy(slices_ref, slab_raw, load_sem.at[0])
    slab_load.start()
    meas_loads = [
        pltpu.make_async_copy(piece_of(zh, c), meas_raw.at[0, c], load_sem.at[1 + c])
        for c in range(3)
    ]
    for load in meas_loads:
        load.start()

    fy = table_ref[0, chosen_ref[0]]
    fx = table_ref[1, chosen_ref[0]]
    freq[0:1, :] = jnp.full((1, LANES), fy, F32)
    freq[1:2, :] = jnp.full((1, LANES), fx, F32)

    slab_load.wait()
    slabs = (near, far)
    for i in range(2):
        slab_wide[...] = slab_raw[i].astype(F32)
        for k in range(2):
            lanes = slice(k * LANES, (k + 1) * LANES)
            unit = join(slab_wide[:, 0, lanes], slab_wide[:, 1, lanes])
            slabs[i][mine + flip(k, 2)] = unit.astype(BF16)

    build_taps(zh, taps_ref, line, wf, wa, rf, ra)

    def waves(t, ref):
        vy = ref[0:1, :]
        vx = ref[1:2, :]
        unit = lax.broadcasted_iota(jnp.int32, (16, LANES), 0)
        pos_r = (r * ROWS + lax.broadcasted_iota(jnp.int32, (ROWS, LANES), 0)).astype(F32)
        pos_c = (flip(unit, 16) * LANES + lax.broadcasted_iota(jnp.int32, (16, LANES), 1)).astype(F32)
        turn_r = (vy * pos_r) * (1.0 / length)
        turn_c = (vx * pos_c) * (1.0 / length)
        ang_r = (2.0 * math.pi) * (turn_r - jnp.floor(turn_r + 0.5))
        ang_c = (2.0 * math.pi) * (turn_c - jnp.floor(turn_c + 0.5))
        cr, sr = jnp.cos(ang_r), jnp.sin(ang_r)
        cc, sc = jnp.cos(ang_c), jnp.sin(ang_c)
        for u in range(UNITS):
            re, im = times(cr, sr, cc[u : u + 1, :], sc[u : u + 1, :])
            inc[t, u, :, 0:LANES] = re
            inc[t, u, :, LANES:] = im

    waves(0, freq)
    for t in range(4):
        field[t, 0] = jnp.zeros((ROWS, 2 * LANES), BF16)
        field[t, UNITS + 1] = jnp.zeros((ROWS, 2 * LANES), BF16)

    @pl.when(jnp.logical_not(has_up))
    def _():
        halo[:, :, :, 0:ROWS, :] = jnp.zeros((4, 2, UNITS, ROWS, 2 * LANES), BF16)

    @pl.when(jnp.logical_not(has_dn))
    def _():
        halo[:, :, :, 2 * ROWS :, :] = jnp.zeros((4, 2, UNITS, ROWS, 2 * LANES), BF16)

    for load in meas_loads:
        load.wait()

    pl.semaphore_wait(barrier, 4 + has_up.astype(jnp.int32) + has_dn.astype(jnp.int32))

    def remote(src, dst, send_sem, recv_sem, to):
        return pltpu.make_async_remote_copy(
            src_ref=src,
            dst_ref=dst,
            send_sem=send_sem,
            recv_sem=recv_sem,
            device_id=to,
            device_id_type=MESH,
        )

    def slab_copy(i, k):
        block = slabs[i].at[pl.ds(mine, 2)]
        to = (r, 4 * zh + lax.rem(x + k, 4))
        return remote(block, block, slab_send.at[i, k - 1], slab_recv.at[i, k - 1], to)

    def slab_wait(i, k):
        block = slabs[i].at[pl.ds(first_of(lax.rem(x + 4 - k, 4)), 2)]
        remote(block, block, slab_send.at[i, k - 1], slab_recv.at[i, k - 1], (r, pair)).wait_recv()

    edges = [
        remote(slabs[i].at[7], slabs[i].at[8], edge_send.at[i], edge_recv.at[i], (r, pair))
        for i in range(2)
    ]
    freq_copy = remote(freq, other_freq, freq_send, freq_recv, (r, pair))
    meas_copies = [
        remote(piece_of(1 - zh, c), meas_raw.at[1, c], meas_send.at[c], meas_recv.at[c], (r, pair))
        for c in range(3)
    ]

    owner = mine == 6
    relay = mine == 0

    def relay_copy(i, k):
        to = (r, 4 * zh + lax.rem(x + k, 4))
        margin = slabs[i].at[8]
        return remote(margin, margin, relay_send.at[i, k - 1], relay_recv.at[i], to)

    def margin_wait(i):
        @pl.when(jnp.logical_not(relay))
        def _():
            relay_copy(i, 1).wait_recv()

    def meas_start():
        for copy in meas_copies:
            copy.start()

    freq_copy.start()

    @pl.when(owner)
    def _():
        edges[0].start()
        edges[1].start()

    for k in range(1, 4):
        slab_copy(0, k).start()
    pl.when(jnp.logical_not(owner))(meas_start)
    for k in range(1, 4):
        slab_copy(1, k).start()

    def halo_copy(s, t, c, down):
        lo = 0 if down else 2 * ROWS
        i = 0 if down else 1
        u0, u1 = PARTS[s][c]
        return remote(
            halo.at[s, t, u0:u1, ROWS : 2 * ROWS, :],
            halo.at[s, t, u0:u1, lo : lo + ROWS, :],
            halo_send.at[s, t, c, i],
            halo_recv.at[s, t, c, i],
            (dn if down else up, a),
        )

    def halo_start(s, t, c):
        @pl.when(has_dn)
        def _():
            halo_copy(s, t, c, True).start()

        @pl.when(has_up)
        def _():
            halo_copy(s, t, c, False).start()

    def halo_wait(s, t, c):
        @pl.when(has_up)
        def _():
            halo_copy(s, t, c, True).wait_recv()

        @pl.when(has_dn)
        def _():
            halo_copy(s, t, c, False).wait_recv()

    def halo_done(s, t, c):
        @pl.when(has_dn)
        def _():
            halo_copy(s, t, c, True).wait_send()

        @pl.when(has_up)
        def _():
            halo_copy(s, t, c, False).wait_send()

    def columns(t, w, u0, u1):
        acc = None
        for j in range(3):
            lhs = field[t, u0 + j : u1 + j].reshape((u1 - u0) * ROWS, 2 * LANES)
            term = jnp.dot(lhs, w[j], preferred_element_type=F32)
            acc = term if acc is None else acc + term
        return acc.astype(BF16).reshape(u1 - u0, ROWS, 2 * LANES)

    def own(s, t, u0, u1, value):
        halo[s, t, u0:u1, ROWS : 2 * ROWS, :] = value

    def enter(t, units, groups, c):
        for u in range(*units):
            re, im = times(*parts(near[u]), *parts(inc[t, u]))
            field[2 + t, u + 1] = join(re, im).astype(BF16)
        for u0, u1 in groups:
            own(0, t, u0, u1, columns(2 + t, wf, u0, u1))
        halo_start(0, t, c)

    def second(t, groups, c):
        halo_wait(0, t, c)
        for u in range(*PARTS[0][c]):
            re, im = row_correlate(rf, halo[0, t, u])
            value = join(re, im).astype(BF16)
            inner[t, u] = value
            re, im = times(*parts(far[u]), *parts(value))
            field[t, u + 1] = join(re, im).astype(BF16)
        for u0, u1 in groups:
            own(1, t, u0, u1, columns(t, wf, u0, u1))
        halo_start(1, t, c)

    def compare(t, c):
        meas_wide[...] = meas_raw[t, c].astype(F32)
        for k in range(3):
            u = 3 * c + k
            re, im = row_correlate(rf, halo[1, t, u])
            value = join(re, im).astype(BF16)
            lanes = pl.ds(pl.multiple_of(flip(k, 3) * LANES, LANES), LANES)
            target = join(meas_wide[:, 0, lanes], meas_wide[:, 1, lanes])
            halo[2, t, u, ROWS : 2 * ROWS, :] = (value.astype(F32) - target).astype(BF16)
        halo_start(2, t, c)

    def back(s, t, c):
        halo_wait(s, t, c)
        for u in range(*PARTS[s][c]):
            re, im = row_correlate(ra, halo[s, t, u])
            field[t, u + 1] = join(re, im).astype(BF16)

    def add(t, total, pack, u0, u1, re, im):
        grad = join(re, im)
        if t == 0:
            total[u0:u1] = grad
        else:
            grad = grad + total[u0:u1]
            total[u0:u1] = grad
            pack[u0:u1] = grad.astype(BF16)

    def back_far(t):
        def piece(c):
            u0, u1 = PARTS[3][c]
            br, bi = parts(columns(t, wa, u0, u1))
            re, im = conj_times(*parts(far[u0:u1]), br, bi)
            own(3, t, u0, u1, join(re, im).astype(BF16))
            halo_start(3, t, c)
            re, im = conj_times(*parts(inner[t, u0:u1]), br, bi)
            add(t, sum_far, pack_far, u0, u1, re, im)

        back(2, t, 0)
        back(2, t, 1)
        piece(0)
        back(2, t, 2)
        piece(1)
        piece(2)

    def back_near(t):
        def piece(c):
            u0, u1 = PARTS[3][c]
            br, bi = parts(columns(t, wa, u0, u1))
            re, im = conj_times(*parts(inc[t, u0:u1]), br, bi)
            add(t, sum_near, pack_near, u0, u1, re, im)

        back(3, t, 0)
        back(3, t, 1)
        piece(0)
        back(3, t, 2)
        piece(1)
        piece(2)

    grads = ((pack_near, got_near, sum_near, out_near), (pack_far, got_far, sum_far, out_far))

    def grad_copy(i, k):
        to = lax.rem(x + k, 4)
        src = grads[i][0].at[pl.ds(first_of(to), 2)]
        dst = grads[i][1].at[k - 1]
        return remote(src, dst, grad_send.at[i, k - 1], grad_recv.at[i, k - 1], (r, 4 * zh + to))

    def finish(i):
        _, got, total, out = grads[i]
        for k in range(1, 4):
            grad_copy(i, k).wait_recv()
        for j in range(2):
            at = flip(j, 2)
            value = total[mine + at]
            for k in range(3):
                value = value + got[k, at].astype(F32)
            out[:, 0, j * LANES : (j + 1) * LANES] = value[:, :LANES]
            out[:, 1, j * LANES : (j + 1) * LANES] = value[:, LANES:]

    early = ((0, 4), (4, 7))
    for k in range(1, 4):
        slab_wait(0, k)
    pl.when(owner)(meas_start)
    enter(0, (0, 8), early, 0)
    freq_copy.wait_recv()
    waves(1, other_freq)
    enter(1, (0, 8), early, 0)

    @pl.when(relay)
    def _():
        for i in range(2):
            edges[i].wait_recv()
            for k in range(1, 4):
                relay_copy(i, k).start()

    for k in range(1, 4):
        slab_wait(1, k)
    early = ((0, 3), (3, 6))
    second(0, early, 0)
    margin_wait(0)
    enter(0, (8, 9), ((7, 9),), 1)
    enter(1, (8, 9), ((7, 9),), 1)
    second(1, early, 0)
    margin_wait(1)
    second(0, ((6, 9),), 1)
    second(1, ((6, 9),), 1)
    halo_wait(1, 0, 0)
    compare(0, 0)
    compare(0, 1)
    halo_wait(1, 1, 0)
    for c in range(2):
        meas_copies[c].wait_recv()
        compare(1, c)
    halo_wait(1, 0, 1)
    compare(0, 2)
    halo_wait(1, 1, 1)
    meas_copies[2].wait_recv()
    compare(1, 2)
    back_far(0)
    back_far(1)
    for k in range(1, 4):
        grad_copy(1, k).start()
    back_near(0)
    back_near(1)
    for k in range(1, 4):
        grad_copy(0, k).start()
    finish(1)
    finish(0)

    for i in range(2):
        for k in range(1, 4):
            slab_copy(i, k).wait_send()
            grad_copy(i, k).wait_send()

        @pl.when(owner)
        def _():
            edges[i].wait_send()

        @pl.when(relay)
        def _():
            for k in range(1, 4):
                relay_copy(i, k).wait_send()

    freq_copy.wait_send()
    for copy in meas_copies:
        copy.wait_send()
    for s in range(4):
        for t in range(2):
            for c in range(len(PARTS[s])):
                halo_done(s, t, c)


def local(rows_n, measured, slices, kernel_taps, angle_freq, chosen):
    length = measured.shape[3]
    unit = (ROWS, 2 * LANES)
    vmem = pl.BlockSpec(memory_space=pltpu.VMEM)
    smem = pl.BlockSpec(memory_space=pltpu.SMEM)
    place = pl.BlockSpec(memory_space=pl.ANY)
    dma = pltpu.SemaphoreType.DMA
    out = jax.ShapeDtypeStruct((ROWS, 2, 2 * LANES), F32)
    return pl.pallas_call(
        functools.partial(kernel, rows_n, length),
        out_shape=(out, out),
        in_specs=[smem, smem, vmem, place, place],
        out_specs=(vmem, vmem),
        scratch_shapes=[
            pltpu.VMEM((2, ROWS, 2, 2 * LANES), BF16),
            pltpu.VMEM((ROWS, 2, 2 * LANES), F32),
            pltpu.VMEM((2, 3, ROWS, 2, PIECE), BF16),
            pltpu.VMEM((ROWS, 2, PIECE), F32),
            pltpu.VMEM((UNITS,) + unit, BF16),
            pltpu.VMEM((UNITS,) + unit, BF16),
            pltpu.VMEM((2, LANES), F32),
            pltpu.VMEM((2, LANES), F32),
            pltpu.VMEM((8, 4 * LANES), F32),
            pltpu.VMEM((3, 2 * LANES, 2 * LANES), BF16),
            pltpu.VMEM((3, 2 * LANES, 2 * LANES), BF16),
            pltpu.VMEM((2 * ROWS, LANES), BF16),
            pltpu.VMEM((2 * ROWS, LANES), BF16),
            pltpu.VMEM((2, UNITS) + unit, F32),
            pltpu.VMEM((2, UNITS) + unit, BF16),
            pltpu.VMEM((4, UNITS + 2) + unit, BF16),
            pltpu.VMEM((4, 2, UNITS, 3 * ROWS, 2 * LANES), BF16),
            pltpu.VMEM((UNITS,) + unit, F32),
            pltpu.VMEM((UNITS,) + unit, F32),
            pltpu.VMEM((UNITS,) + unit, BF16),
            pltpu.VMEM((UNITS,) + unit, BF16),
            pltpu.VMEM((3, 2) + unit, BF16),
            pltpu.VMEM((3, 2) + unit, BF16),
            dma((4,)),
            dma((2, 3)),
            dma((2, 3)),
            dma((2,)),
            dma((2,)),
            dma((2, 3)),
            dma((2,)),
            dma,
            dma,
            dma((3,)),
            dma((3,)),
            dma((4, 2, 3, 2)),
            dma((4, 2, 3, 2)),
            dma((2, 3)),
            dma((2, 3)),
        ],
        compiler_params=pltpu.CompilerParams(collective_id=0, has_side_effects=True),
    )(chosen, angle_freq.T, kernel_taps, slices, measured)


def solution(mesh):
    return jax.shard_map(
        functools.partial(local, mesh.shape["rows"]),
        mesh=mesh,
        in_specs=(P("ang", "rows", None, None), P(None, "rows", None, "ang"), P(), P(), P("ang")),
        out_specs=(P("rows", None, "ang"), P("rows", None, "ang")),
        check_vma=False,
    )
```

time: 78.4 us -> 63.6 us (0.81)
  Pallas kernels: 71 us -> 59.9 us
  local copies, waits for them, and re-layouts: 5.87 us -> 2.14 us
    pallas_call x1, Pallas kernels: 71 us -> 59.9 us  [local(): pl.pallas_call(functools.partial(kernel, rows_n, length), out_shape=(out,...]
    reshape x4 -> x0, local copies, waits for them, and re-layouts: 2.51 us -> none  [the longest x3 1.64 us: place(): grad.reshape(2, ROWS, 2, LANES).transpose(1, 2, 0, 3)]
    squeeze x2 -> x0, local copies, waits for them, and re-layouts: 1.27 us -> none  [the longest x1 0.64 us: local(): slabs[0]]
    unnamed x9 -> x4, local copies, waits for them, and re-layouts: 1.58 us -> 2.14 us
where the time goes in v2:
time: 63.6 us; the launch traced here: 63.3 us
  Pallas kernels  59.9 us (94%)
  local copies, waits for them, and re-layouts  2.14 us (3%)
  between operations  1.29 us (2%)
    pallas_call x1, Pallas kernels, local(): pl.pallas_call(functools.partial(kernel, rows_n, length), out_shape=(out,...  59.9 us
    unnamed x4, local copies, waits for them, and re-layouts  2.14 us

profile of v2, /device:TPU:32, one launch (start us, length us, event | category | flops | bytes accessed | tf_op | source)
XLA Modules:
  0.0 63.3 jit_solution(12022317146529825816)
XLA Ops:
  1.3 59.9 %shard_map.68 = (f32[32,2,256]{2,1,0:T(2,128)}, f32[32,2,256]{2,1,0:T(2,128)}) custom-call(s32[1]{0:T(128)S(6)} %copy.9.chosen_ref, f32[2,128]{1,0:T(2,128)} %bitcast.1, bf16[2,65]{1,0:T(2,128)(2,1)} %taps_ref.1, bf16[2,32,2,256]{3,2,1,0:T(2,128)(2,1)} %slices_ref.1, bf16[1,32,2,2048]{3,2,1,0:T(2,128)(2,1)} %meas_ref.1), custom_call_target="tpu_custom_call" | custom-call | tf_op jit(solution)/shard_map/pallas_call | solution.py:524
  61.2 0.0 copy-start
  61.2 1.5 %copy.10 = f32[32,2,256]{2,1,0:T(2,128)} copy(f32[32,2,256]{2,1,0:T(2,128)} %get-tuple-element.4) | data formatting | bytes 131072
  62.7 0.0 copy-done
  62.7 0.6 copy.11
Async XLA Ops:
  61.2 1.5 %copy-start = (f32[32,2,256]{2,1,0:T(2,128)S(1)}, f32[32,2,256]{2,1,0:T(2,128)}, u32[]{:S(2)}) copy-start(f32[32,2,256]{2,1,0:T(2,128)} %get-tuple-element.5) | copy-start | bytes 196612

commit v3 on v2

v3 whole, which is shorter than its diff:
```python
import functools
import math

import jax
import jax.numpy as jnp
from jax import lax
from jax.experimental import pallas as pl
from jax.experimental.pallas import tpu as pltpu
from jax.sharding import PartitionSpec as P

MESH = pl.DeviceIdType.MESH
F32 = jnp.float32
BF16 = jnp.bfloat16
ROWS = 32
LANES = 128
UNITS = 9
REACH = 32
TAPS = 65


def build_taps(zh, taps_ref, line, wf, wa, rf, ra):
    line[...] = jnp.zeros_like(line)
    line[0:2, 0:TAPS] = taps_ref[...].astype(F32)
    gr = line[0:1, :]
    gi = line[1:2, :]

    def column(vec, j):
        wide = jnp.broadcast_to(vec, (LANES, 4 * LANES))
        shift = (LANES * (j - 1) - REACH) % (4 * LANES)
        return pltpu.roll(wide, shift, 1, stride=1, stride_axis=0)[:, :LANES]

    for j in range(3):
        re = column(gr, j)
        im = column(gi, j)
        ja = j + zh * (2 - 2 * j)
        jf = 2 - ja
        wa[ja, 0:LANES, 0:LANES] = re.astype(BF16)
        wa[ja, 0:LANES, LANES:] = (-im).astype(BF16)
        wa[ja, LANES:, 0:LANES] = im.astype(BF16)
        wa[ja, LANES:, LANES:] = re.astype(BF16)
        ret = re.T
        imt = im.T
        wf[jf, 0:LANES, 0:LANES] = ret.astype(BF16)
        wf[jf, 0:LANES, LANES:] = imt.astype(BF16)
        wf[jf, LANES:, 0:LANES] = (-imt).astype(BF16)
        wf[jf, LANES:, LANES:] = ret.astype(BF16)

    def row(vec, sign):
        narrow = vec[:, :LANES]
        ahead = pltpu.roll(jnp.broadcast_to(narrow, (ROWS, LANES)), 0, 1, stride=1, stride_axis=0)
        back = pltpu.roll(
            jnp.broadcast_to(narrow, (LANES, LANES)), LANES - 2 * REACH, 1, stride=1, stride_axis=0
        )
        return ahead, sign * back.T[0:ROWS, :]

    fr, br = row(gr, 1.0)
    fi, bi = row(gi, -1.0)
    rf[0:ROWS, :] = fr.astype(BF16)
    rf[ROWS:, :] = fi.astype(BF16)
    ra[0:ROWS, :] = br.astype(BF16)
    ra[ROWS:, :] = bi.astype(BF16)


def row_correlate(taps, window):
    both = jnp.dot(taps[:, 0 : 3 * ROWS], window, preferred_element_type=F32)
    re = both[:ROWS, :LANES] - both[ROWS:, LANES:]
    im = both[:ROWS, LANES:] + both[ROWS:, :LANES]
    return re, im


def times(ar, ai, br, bi):
    return ar * br - ai * bi, ar * bi + ai * br


def conj_times(ar, ai, br, bi):
    return ar * br + ai * bi, ar * bi - ai * br


def join(re, im):
    return jnp.concatenate([re, im], axis=-1)


def parts(value):
    value = value.astype(F32)
    return value[..., :LANES], value[..., LANES:]


SLAB_PARTS = ((0, 8),)
PARTS = ((0, 3), (3, 6), (6, 9))
PIECE = 3 * LANES


def kernel(
    rows_n,
    length,
    chosen_ref,
    table_ref,
    taps_ref,
    slices_ref,
    meas_ref,
    out,
    slab_raw,
    slab_wide,
    meas_raw,
    meas_wide,
    near,
    far,
    freq,
    other_freq,
    line,
    wf,
    wa,
    rf,
    ra,
    inc,
    inner,
    entry,
    first,
    field,
    halo,
    sum_near,
    sum_far,
    pack_near,
    pack_far,
    got_near,
    got_far,
    load_sem,
    slab_send,
    slab_recv,
    edge_send,
    edge_recv,
    relay_send,
    relay_recv,
    freq_send,
    freq_recv,
    meas_send,
    meas_recv,
    halo_send,
    halo_recv,
    grad_send,
    grad_recv,
):
    r = lax.axis_index("rows")
    a = lax.axis_index("ang")
    zh = a // 4
    x = lax.rem(a, 4)
    has_up = r > 0
    has_dn = r < rows_n - 1
    up = lax.rem(r + rows_n - 1, rows_n)
    dn = lax.rem(r + 1, rows_n)
    pair = lax.rem(a + 4, 8)

    def first_of(other_x):
        return 2 * other_x + zh * (6 - 4 * other_x)

    mine = first_of(x)

    def flip(i, n):
        return i + zh * (n - 1 - 2 * i)

    barrier = pltpu.get_barrier_semaphore()
    pl.semaphore_signal(barrier, inc=1, device_id=(r, pair), device_id_type=MESH)
    for k in range(1, 4):
        to = (r, 4 * zh + lax.rem(x + k, 4))
        pl.semaphore_signal(barrier, inc=1, device_id=to, device_id_type=MESH)

    owner = mine == 6
    relay = mine == 0
    end = jnp.logical_or(owner, relay)
    for has, row in ((has_up, up), (has_dn, dn)):

        @pl.when(has)
        def _():
            pl.semaphore_signal(barrier, inc=1, device_id=(row, a), device_id_type=MESH)

        @pl.when(jnp.logical_and(has, end))
        def _():
            pl.semaphore_signal(barrier, inc=1, device_id=(row, pair), device_id_type=MESH)

    def meas_from(half, u):
        block = u + half * (15 - 2 * u)
        return meas_ref.at[0, :, :, pl.ds(pl.multiple_of(block * LANES, LANES), LANES)]

    def meas_to(t, u):
        return meas_raw.at[t, u // 3, :, :, u % 3 * LANES : (u % 3 + 1) * LANES]

    slab_load = pltpu.make_async_copy(slices_ref, slab_raw, load_sem.at[0])
    slab_load.start()
    meas_loads = [
        pltpu.make_async_copy(meas_from(zh, u), meas_to(0, u), load_sem.at[1 + u])
        for u in range(UNITS)
    ]
    for load in meas_loads:
        load.start()

    fy = table_ref[0, chosen_ref[0]]
    fx = table_ref[1, chosen_ref[0]]
    freq[0:1, :] = jnp.full((1, LANES), fy, F32)
    freq[1:2, :] = jnp.full((1, LANES), fx, F32)

    slab_load.wait()

    def slab(i, unit, n):
        if i == 0:
            return near.at[pl.ds(unit, n), ROWS : 2 * ROWS, :]
        return far.at[pl.ds(unit, n)]

    for i in range(2):
        slab_wide[...] = slab_raw[i].astype(F32)
        for k in range(2):
            lanes = slice(k * LANES, (k + 1) * LANES)
            unit = join(slab_wide[:, 0, lanes], slab_wide[:, 1, lanes])
            slab(i, mine + flip(k, 2), 1)[...] = unit.astype(BF16)[None]

    build_taps(zh, taps_ref, line, wf, wa, rf, ra)

    def waves(t, ref):
        vy = ref[0:1, :]
        vx = ref[1:2, :]
        unit = lax.broadcasted_iota(jnp.int32, (16, LANES), 0)
        wide = lax.broadcasted_iota(jnp.int32, (3 * ROWS, LANES), 0)
        pos_r = ((r - 1) * ROWS + wide).astype(F32)
        pos_c = (flip(unit, 16) * LANES + lax.broadcasted_iota(jnp.int32, (16, LANES), 1)).astype(F32)
        turn_r = (vy * pos_r) * (1.0 / length)
        turn_c = (vx * pos_c) * (1.0 / length)
        ang_r = (2.0 * math.pi) * (turn_r - jnp.floor(turn_r + 0.5))
        ang_c = (2.0 * math.pi) * (turn_c - jnp.floor(turn_c + 0.5))
        cr, sr = jnp.cos(ang_r), jnp.sin(ang_r)
        cc, sc = jnp.cos(ang_c), jnp.sin(ang_c)
        for u in range(UNITS):
            re, im = times(cr, sr, cc[u : u + 1, :], sc[u : u + 1, :])
            inc[t, u, :, 0:LANES] = re
            inc[t, u, :, LANES:] = im

    waves(0, freq)
    for t in range(2):
        entry[t, 0] = jnp.zeros((3 * ROWS, 2 * LANES), BF16)
        entry[t, UNITS + 1] = jnp.zeros((3 * ROWS, 2 * LANES), BF16)
        field[t, 0] = jnp.zeros((ROWS, 2 * LANES), BF16)
        field[t, UNITS + 1] = jnp.zeros((ROWS, 2 * LANES), BF16)

    @pl.when(jnp.logical_not(has_up))
    def _():
        near[:, 0:ROWS, :] = jnp.zeros((UNITS, ROWS, 2 * LANES), BF16)
        halo[:, :, :, 0:ROWS, :] = jnp.zeros((3, 2, UNITS, ROWS, 2 * LANES), BF16)

    @pl.when(jnp.logical_not(has_dn))
    def _():
        near[:, 2 * ROWS :, :] = jnp.zeros((UNITS, ROWS, 2 * LANES), BF16)
        halo[:, :, :, 2 * ROWS :, :] = jnp.zeros((3, 2, UNITS, ROWS, 2 * LANES), BF16)

    for load in meas_loads:
        load.wait()

    beside = has_up.astype(jnp.int32) + has_dn.astype(jnp.int32)
    pl.semaphore_wait(barrier, 4 + beside * (1 + end.astype(jnp.int32)))

    def remote(src, dst, send_sem, recv_sem, to):
        return pltpu.make_async_remote_copy(
            src_ref=src,
            dst_ref=dst,
            send_sem=send_sem,
            recv_sem=recv_sem,
            device_id=to,
            device_id_type=MESH,
        )

    def slab_copy(i, k):
        block = slab(i, mine, 2)
        to = (r, 4 * zh + lax.rem(x + k, 4))
        return remote(block, block, slab_send.at[i, k - 1], slab_recv.at[i, k - 1], to)

    def slab_wait(i, k):
        block = slab(i, first_of(lax.rem(x + 4 - k, 4)), 2)
        remote(block, block, slab_send.at[i, k - 1], slab_recv.at[i, k - 1], (r, pair)).wait_recv()

    def edge_copy(i, d):
        lo = ROWS - ROWS * d
        dst = near.at[8:9, lo : lo + ROWS, :] if i == 0 else slab(1, 8, 1)
        row = (up, r, dn)[d + 1]
        sems = edge_send.at[i, d + 1], edge_recv.at[i, d + 1]
        return remote(slab(i, 7, 1), dst, *sems, (row, pair))

    def edge_each(sending, act):
        act(edge_copy(0, 0))
        act(edge_copy(1, 0))
        for d in (-1, 1):
            @pl.when(has_up if (d < 0) == sending else has_dn)
            def _():
                act(edge_copy(0, d))

    freq_copy = remote(freq, other_freq, freq_send, freq_recv, (r, pair))
    meas_copies = [
        remote(meas_from(1 - zh, u), meas_to(1, u), meas_send.at[u], meas_recv.at[u], (r, pair))
        for u in range(UNITS)
    ]

    def relay_copy(i, k):
        to = (r, 4 * zh + lax.rem(x + k, 4))
        margin = (near, far)[i].at[8]
        return remote(margin, margin, relay_send.at[i, k - 1], relay_recv.at[i], to)

    def margin_wait(i):
        @pl.when(jnp.logical_not(relay))
        def _():
            relay_copy(i, 1).wait_recv()

    def meas_start(*pieces):
        for u in pieces:
            meas_copies[u].start()

    freq_copy.start()

    @pl.when(owner)
    def _():
        edge_each(True, lambda copy: copy.start())

    for k in range(1, 4):
        slab_copy(0, k).start()

    @pl.when(jnp.logical_not(owner))
    def _():
        meas_start(*range(UNITS))

    for k in range(1, 4):
        slab_copy(1, k).start()

    def halo_copy(s, t, c, down):
        lo = 0 if down else 2 * ROWS
        i = 0 if down else 1
        u0, u1 = SLAB_PARTS[c] if s == 0 else PARTS[c]
        ref = near if s == 0 else halo.at[s - 1, t]
        return remote(
            ref.at[u0:u1, ROWS : 2 * ROWS, :],
            ref.at[u0:u1, lo : lo + ROWS, :],
            halo_send.at[s, t, c, i],
            halo_recv.at[s, t, c, i],
            (dn if down else up, a),
        )

    def halo_each(s, t, c, sending, act):
        @pl.when(has_dn if sending else has_up)
        def _():
            act(halo_copy(s, t, c, True))

        @pl.when(has_up if sending else has_dn)
        def _():
            act(halo_copy(s, t, c, False))

    def halo_start(s, t, c):
        halo_each(s, t, c, True, lambda copy: copy.start())

    def halo_wait(s, t, c):
        halo_each(s, t, c, False, lambda copy: copy.wait_recv())

    def halo_done(s, t, c):
        halo_each(s, t, c, True, lambda copy: copy.wait_send())

    def columns(ref, w, u0, u1):
        rows = ref.shape[1]
        acc = None
        for j in range(3):
            lhs = ref[u0 + j : u1 + j].reshape((u1 - u0) * rows, 2 * LANES)
            term = jnp.dot(lhs, w[j], preferred_element_type=F32)
            acc = term if acc is None else acc + term
        return acc.astype(BF16).reshape(u1 - u0, rows, 2 * LANES)

    def own(s, t, u0, u1, value):
        halo[s - 1, t, u0:u1, ROWS : 2 * ROWS, :] = value

    def enter(t):
        for u in range(UNITS):
            re, im = times(*parts(near[u]), *parts(inc[t, u]))
            entry[t, u + 1] = join(re, im).astype(BF16)
        for u0, u1 in PARTS:
            first[t, u0:u1] = columns(entry.at[t], wf, u0, u1)

    def second(t):
        for u in range(UNITS):
            re, im = row_correlate(rf, first[t, u])
            value = join(re, im).astype(BF16)
            inner[t, u] = value
            re, im = times(*parts(far[u]), *parts(value))
            field[t, u + 1] = join(re, im).astype(BF16)
        for c, (u0, u1) in enumerate(PARTS):
            own(1, t, u0, u1, columns(field.at[t], wf, u0, u1))
            halo_start(1, t, c)

    def compare(t, c):
        halo_wait(1, t, c)
        meas_wide[...] = meas_raw[t, c].astype(F32)
        for k in range(3):
            u = 3 * c + k
            re, im = row_correlate(rf, halo[0, t, u])
            value = join(re, im).astype(BF16)
            lanes = slice(k * LANES, (k + 1) * LANES)
            target = join(meas_wide[:, 0, lanes], meas_wide[:, 1, lanes])
            halo[1, t, u, ROWS : 2 * ROWS, :] = (value.astype(F32) - target).astype(BF16)
        halo_start(2, t, c)

    def back(s, t, c):
        halo_wait(s, t, c)
        for u in range(*PARTS[c]):
            re, im = row_correlate(ra, halo[s - 1, t, u])
            field[t, u + 1] = join(re, im).astype(BF16)

    def add(t, total, pack, u0, u1, re, im):
        grad = join(re, im)
        if t == 0:
            total[u0:u1] = grad
        else:
            grad = grad + total[u0:u1]
            total[u0:u1] = grad
            pack[u0:u1] = grad.astype(BF16)

    def back_far(t):
        def piece(c):
            u0, u1 = PARTS[c]
            br, bi = parts(columns(field.at[t], wa, u0, u1))
            re, im = conj_times(*parts(far[u0:u1]), br, bi)
            own(3, t, u0, u1, join(re, im).astype(BF16))
            halo_start(3, t, c)
            re, im = conj_times(*parts(inner[t, u0:u1]), br, bi)
            add(t, sum_far, pack_far, u0, u1, re, im)

        back(2, t, 0)
        back(2, t, 1)
        piece(0)
        back(2, t, 2)
        piece(1)
        piece(2)

    def back_near(t):
        def piece(c):
            u0, u1 = PARTS[c]
            br, bi = parts(columns(field.at[t], wa, u0, u1))
            re, im = conj_times(*parts(inc[t, u0:u1, ROWS : 2 * ROWS]), br, bi)
            add(t, sum_near, pack_near, u0, u1, re, im)

        back(3, t, 0)
        back(3, t, 1)
        piece(0)
        back(3, t, 2)
        piece(1)
        piece(2)

    grads = ((pack_near, got_near, sum_near), (pack_far, got_far, sum_far))

    def grad_copy(i, k):
        to = lax.rem(x + k, 4)
        src = grads[i][0].at[pl.ds(first_of(to), 2)]
        dst = grads[i][1].at[k - 1]
        return remote(src, dst, grad_send.at[i, k - 1], grad_recv.at[i, k - 1], (r, 4 * zh + to))

    def finish(i):
        _, got, total = grads[i]
        for k in range(1, 4):
            grad_copy(i, k).wait_recv()
        for j in range(2):
            at = flip(j, 2)
            value = total[mine + at]
            for k in range(3):
                value = value + got[k, at].astype(F32)
            out[i, :, 0, j * LANES : (j + 1) * LANES] = value[:, :LANES]
            out[i, :, 1, j * LANES : (j + 1) * LANES] = value[:, LANES:]

    for k in range(1, 4):
        slab_wait(0, k)
    halo_start(0, 0, 0)

    @pl.when(owner)
    def _():
        meas_start(*range(UNITS))

    @pl.when(relay)
    def _():
        edge_each(False, lambda copy: copy.wait_recv())
        for i in range(2):
            for k in range(1, 4):
                relay_copy(i, k).start()

    for k in range(1, 4):
        slab_wait(1, k)
    halo_wait(0, 0, 0)
    margin_wait(0)
    enter(0)
    freq_copy.wait_recv()
    waves(1, other_freq)
    enter(1)
    margin_wait(1)
    second(0)
    second(1)
    for c in range(3):
        compare(0, c)
    for c in range(3):
        for u in range(*PARTS[c]):
            meas_copies[u].wait_recv()
        compare(1, c)
    back_far(0)
    back_far(1)
    for k in range(1, 4):
        grad_copy(1, k).start()
    back_near(0)
    back_near(1)
    for k in range(1, 4):
        grad_copy(0, k).start()
    finish(1)
    finish(0)

    for i in range(2):
        for k in range(1, 4):
            slab_copy(i, k).wait_send()
            grad_copy(i, k).wait_send()

        @pl.when(owner)
        def _():
            if i == 0:
                edge_each(True, lambda copy: copy.wait_send())

        @pl.when(relay)
        def _():
            for k in range(1, 4):
                relay_copy(i, k).wait_send()

    freq_copy.wait_send()
    for copy in meas_copies:
        copy.wait_send()
    halo_done(0, 0, 0)
    for s in range(1, 4):
        for t in range(2):
            for c in range(3):
                halo_done(s, t, c)


def local(rows_n, measured, slices, kernel_taps, angle_freq, chosen):
    length = measured.shape[3]
    unit = (ROWS, 2 * LANES)
    wide = (3 * ROWS, 2 * LANES)
    vmem = pl.BlockSpec(memory_space=pltpu.VMEM)
    smem = pl.BlockSpec(memory_space=pltpu.SMEM)
    place = pl.BlockSpec(memory_space=pl.ANY)
    dma = pltpu.SemaphoreType.DMA
    grads = pl.pallas_call(
        functools.partial(kernel, rows_n, length),
        out_shape=jax.ShapeDtypeStruct((2, ROWS, 2, 2 * LANES), F32),
        in_specs=[smem, smem, vmem, place, place],
        out_specs=vmem,
        scratch_shapes=[
            pltpu.VMEM((2, ROWS, 2, 2 * LANES), BF16),
            pltpu.VMEM((ROWS, 2, 2 * LANES), F32),
            pltpu.VMEM((2, 3, ROWS, 2, PIECE), BF16),
            pltpu.VMEM((ROWS, 2, PIECE), F32),
            pltpu.VMEM((UNITS,) + wide, BF16),
            pltpu.VMEM((UNITS,) + unit, BF16),
            pltpu.VMEM((2, LANES), F32),
            pltpu.VMEM((2, LANES), F32),
            pltpu.VMEM((8, 4 * LANES), F32),
            pltpu.VMEM((3, 2 * LANES, 2 * LANES), BF16),
            pltpu.VMEM((3, 2 * LANES, 2 * LANES), BF16),
            pltpu.VMEM((2 * ROWS, LANES), BF16),
            pltpu.VMEM((2 * ROWS, LANES), BF16),
            pltpu.VMEM((2, UNITS) + wide, F32),
            pltpu.VMEM((2, UNITS) + unit, BF16),
            pltpu.VMEM((2, UNITS + 2) + wide, BF16),
            pltpu.VMEM((2, UNITS) + wide, BF16),
            pltpu.VMEM((2, UNITS + 2) + unit, BF16),
            pltpu.VMEM((3, 2, UNITS) + wide, BF16),
            pltpu.VMEM((UNITS,) + unit, F32),
            pltpu.VMEM((UNITS,) + unit, F32),
            pltpu.VMEM((UNITS,) + unit, BF16),
            pltpu.VMEM((UNITS,) + unit, BF16),
            pltpu.VMEM((3, 2) + unit, BF16),
            pltpu.VMEM((3, 2) + unit, BF16),
            dma((1 + UNITS,)),
            dma((2, 3)),
            dma((2, 3)),
            dma((2, 3)),
            dma((2, 3)),
            dma((2, 3)),
            dma((2,)),
            dma,
            dma,
            dma((UNITS,)),
            dma((UNITS,)),
            dma((4, 2, 3, 2)),
            dma((4, 2, 3, 2)),
            dma((2, 3)),
            dma((2, 3)),
        ],
        compiler_params=pltpu.CompilerParams(collective_id=0, has_side_effects=True),
    )(chosen, angle_freq.T, kernel_taps, slices, measured)
    return grads[0], grads[1]


def solution(mesh):
    return jax.shard_map(
        functools.partial(local, mesh.shape["rows"]),
        mesh=mesh,
        in_specs=(P("ang", "rows", None, None), P(None, "rows", None, "ang"), P(), P(), P("ang")),
        out_specs=(P("rows", None, "ang"), P("rows", None, "ang")),
        check_vma=False,
    )
```

time: 63.6 us -> 61.9 us (0.973)
  the two profiles are of different devices: /device:TPU:32 before, /device:TPU:224 now
where the time goes in v3:
time: 61.9 us; the launch traced here: 61.6 us
  Pallas kernels  58.8 us (95%)
  local copies, waits for them, and re-layouts  1.53 us (2%)
  between operations  1.29 us (2%)
    pallas_call x1, Pallas kernels, local(): pl.pallas_call(functools.partial(kernel, rows_n, length), out_shape=jax.S...  58.8 us
    squeeze x1, local copies, waits for them, and re-layouts, local(): return (grads[0], grads[1])  1.53 us

profile of v3, /device:TPU:224, one launch (start us, length us, event | category | flops | bytes accessed | tf_op | source)
XLA Modules:
  0.0 61.6 jit_solution(9630600368197106391)
XLA Ops:
  1.3 58.8 %shard_map.68 = f32[2,32,2,256]{3,2,1,0:T(2,128)} custom-call(s32[1]{0:T(128)S(6)} %copy.7.chosen_ref, f32[2,128]{1,0:T(2,128)} %bitcast.5, bf16[2,65]{1,0:T(2,128)(2,1)} %taps_ref.1, bf16[2,32,2,256]{3,2,1,0:T(2,128)(2,1)} %slices_ref.1, bf16[1,32,2,2048]{3,2,1,0:T(2,128)(2,1)} %meas_ref.1), custom_call_target="tpu_custom_call" | custom-call | tf_op jit(solution)/shard_map/pallas_call | solution.py:543
  60.1 1.5 %slice_bitcast_fusion = (f32[32,2,256]{2,1,0:T(2,128)}, f32[32,2,256]{2,1,0:T(2,128)}) fusion(f32[2,32,2,256]{3,2,1,0:T(2,128)} %shard_map.68), kind=kLoop, calls=%fused_computation | loop fusion | bytes 262144 | tf_op jit(solution)/shard_map/squeeze | solution.py:592

commit v4 on v3

--- a/solution.py
+++ b/solution.py
@@ -85,7 +85,7 @@
     return value[..., :LANES], value[..., LANES:]
 
 
-SLAB_PARTS = ((0, 8),)
+SLAB_PARTS = ((0, 4), (4, 8))
 PARTS = ((0, 3), (3, 6), (6, 9))
 PIECE = 3 * LANES
 
@@ -124,6 +124,7 @@
     pack_far,
     got_near,
     got_far,
+    result,
     load_sem,
     slab_send,
     slab_recv,
@@ -177,21 +178,13 @@
         def _():
             pl.semaphore_signal(barrier, inc=1, device_id=(row, pair), device_id_type=MESH)
 
-    def meas_from(half, u):
-        block = u + half * (15 - 2 * u)
-        return meas_ref.at[0, :, :, pl.ds(pl.multiple_of(block * LANES, LANES), LANES)]
-
-    def meas_to(t, u):
-        return meas_raw.at[t, u // 3, :, :, u % 3 * LANES : (u % 3 + 1) * LANES]
+    def meas_from(half):
+        return meas_ref.at[0, :, :, pl.ds(pl.multiple_of(7 * half * LANES, LANES), UNITS * LANES)]
 
     slab_load = pltpu.make_async_copy(slices_ref, slab_raw, load_sem.at[0])
     slab_load.start()
-    meas_loads = [
-        pltpu.make_async_copy(meas_from(zh, u), meas_to(0, u), load_sem.at[1 + u])
-        for u in range(UNITS)
-    ]
-    for load in meas_loads:
-        load.start()
+    meas_load = pltpu.make_async_copy(meas_from(zh), meas_raw.at[0], load_sem.at[1])
+    meas_load.start()
 
     fy = table_ref[0, chosen_ref[0]]
     fx = table_ref[1, chosen_ref[0]]
@@ -232,13 +225,6 @@
             inc[t, u, :, 0:LANES] = re
             inc[t, u, :, LANES:] = im
 
-    waves(0, freq)
-    for t in range(2):
-        entry[t, 0] = jnp.zeros((3 * ROWS, 2 * LANES), BF16)
-        entry[t, UNITS + 1] = jnp.zeros((3 * ROWS, 2 * LANES), BF16)
-        field[t, 0] = jnp.zeros((ROWS, 2 * LANES), BF16)
-        field[t, UNITS + 1] = jnp.zeros((ROWS, 2 * LANES), BF16)
-
     @pl.when(jnp.logical_not(has_up))
     def _():
         near[:, 0:ROWS, :] = jnp.zeros((UNITS, ROWS, 2 * LANES), BF16)
@@ -248,9 +234,6 @@
     def _():
         near[:, 2 * ROWS :, :] = jnp.zeros((UNITS, ROWS, 2 * LANES), BF16)
         halo[:, :, :, 2 * ROWS :, :] = jnp.zeros((3, 2, UNITS, ROWS, 2 * LANES), BF16)
-
-    for load in meas_loads:
-        load.wait()
 
     beside = has_up.astype(jnp.int32) + has_dn.astype(jnp.int32)
     pl.semaphore_wait(barrier, 4 + beside * (1 + end.astype(jnp.int32)))
@@ -290,10 +273,20 @@
                 act(edge_copy(0, d))
 
     freq_copy = remote(freq, other_freq, freq_send, freq_recv, (r, pair))
-    meas_copies = [
-        remote(meas_from(1 - zh, u), meas_to(1, u), meas_send.at[u], meas_recv.at[u], (r, pair))
-        for u in range(UNITS)
-    ]
+    def meas_copy(c):
+        half = 1 - zh
+        at = (c + half * (2 - 2 * c)) * PIECE
+        lanes = pl.ds(pl.multiple_of(at, LANES), PIECE)
+        start = pl.multiple_of(7 * half * LANES + at, LANES)
+        src = meas_ref.at[0, :, :, pl.ds(start, PIECE)]
+        dst = meas_raw.at[1, :, :, lanes]
+        return remote(src, dst, meas_send.at[c], meas_recv.at[c], (r, pair))
+
+    def meas_wait(c):
+        lanes = pl.ds(pl.multiple_of(flip(c, 3) * PIECE, LANES), PIECE)
+        dst = meas_raw.at[1, :, :, lanes]
+        remote(dst, dst, meas_send.at[c], meas_recv.at[c], (r, pair)).wait_recv()
+
 
     def relay_copy(i, k):
         to = (r, 4 * zh + lax.rem(x + k, 4))
@@ -305,10 +298,6 @@
         def _():
             relay_copy(i, 1).wait_recv()
 
-    def meas_start(*pieces):
-        for u in pieces:
-            meas_copies[u].start()
-
     freq_copy.start()
 
     @pl.when(owner)
@@ -320,7 +309,8 @@
 
     @pl.when(jnp.logical_not(owner))
     def _():
-        meas_start(*range(UNITS))
+        for c in range(3):
+            meas_copy(c).start()
 
     for k in range(1, 4):
         slab_copy(1, k).start()
@@ -369,10 +359,18 @@
         halo[s - 1, t, u0:u1, ROWS : 2 * ROWS, :] = value
 
     def enter(t):
-        for u in range(UNITS):
-            re, im = times(*parts(near[u]), *parts(inc[t, u]))
-            entry[t, u + 1] = join(re, im).astype(BF16)
-        for u0, u1 in PARTS:
+        at = 0
+        for c, (u0, u1) in enumerate(PARTS):
+            if t == 0:
+                if c < 2:
+                    halo_wait(0, 0, c)
+                else:
+                    margin_wait(0)
+            ahead = min(u1 + 1, UNITS)
+            for u in range(at, ahead):
+                re, im = times(*parts(near[u]), *parts(inc[t, u]))
+                entry[t, u + 1] = join(re, im).astype(BF16)
+            at = ahead
             first[t, u0:u1] = columns(entry.at[t], wf, u0, u1)
 
     def second(t):
@@ -388,12 +386,13 @@
 
     def compare(t, c):
         halo_wait(1, t, c)
-        meas_wide[...] = meas_raw[t, c].astype(F32)
+        lanes = pl.ds(pl.multiple_of(flip(c, 3) * PIECE, LANES), PIECE)
+        meas_wide[...] = meas_raw[t, :, :, lanes].astype(F32)
         for k in range(3):
             u = 3 * c + k
             re, im = row_correlate(rf, halo[0, t, u])
             value = join(re, im).astype(BF16)
-            lanes = slice(k * LANES, (k + 1) * LANES)
+            lanes = pl.ds(pl.multiple_of(flip(k, 3) * LANES, LANES), LANES)
             target = join(meas_wide[:, 0, lanes], meas_wide[:, 1, lanes])
             halo[1, t, u, ROWS : 2 * ROWS, :] = (value.astype(F32) - target).astype(BF16)
         halo_start(2, t, c)
@@ -461,16 +460,25 @@
             value = total[mine + at]
             for k in range(3):
                 value = value + got[k, at].astype(F32)
-            out[i, :, 0, j * LANES : (j + 1) * LANES] = value[:, :LANES]
-            out[i, :, 1, j * LANES : (j + 1) * LANES] = value[:, LANES:]
+            result[i, :, 0, j * LANES : (j + 1) * LANES] = value[:, :LANES]
+            result[i, :, 1, j * LANES : (j + 1) * LANES] = value[:, LANES:]
+
+    waves(0, freq)
+    for t in range(2):
+        entry[t, 0] = jnp.zeros((3 * ROWS, 2 * LANES), BF16)
+        entry[t, UNITS + 1] = jnp.zeros((3 * ROWS, 2 * LANES), BF16)
+        field[t, 0] = jnp.zeros((ROWS, 2 * LANES), BF16)
+        field[t, UNITS + 1] = jnp.zeros((ROWS, 2 * LANES), BF16)
 
     for k in range(1, 4):
         slab_wait(0, k)
     halo_start(0, 0, 0)
+    halo_start(0, 0, 1)
 
     @pl.when(owner)
     def _():
-        meas_start(*range(UNITS))
+        for c in range(3):
+            meas_copy(c).start()
 
     @pl.when(relay)
     def _():
@@ -481,20 +489,18 @@
 
     for k in range(1, 4):
         slab_wait(1, k)
-    halo_wait(0, 0, 0)
-    margin_wait(0)
     enter(0)
     freq_copy.wait_recv()
     waves(1, other_freq)
     enter(1)
+    meas_load.wait()
     margin_wait(1)
     second(0)
     second(1)
     for c in range(3):
         compare(0, c)
     for c in range(3):
-        for u in range(*PARTS[c]):
-            meas_copies[u].wait_recv()
+        meas_wait(c)
         compare(1, c)
     back_far(0)
     back_far(1)
@@ -504,8 +510,11 @@
     back_near(1)
     for k in range(1, 4):
         grad_copy(0, k).start()
+    stores = [pltpu.make_async_copy(result.at[i], out.at[i], load_sem.at[2 + i]) for i in range(2)]
     finish(1)
+    stores[1].start()
     finish(0)
+    stores[0].start()
 
     for i in range(2):
         for k in range(1, 4):
@@ -523,9 +532,12 @@
                 relay_copy(i, k).wait_send()
 
     freq_copy.wait_send()
-    for copy in meas_copies:
-        copy.wait_send()
+    for c in range(3):
+        meas_copy(c).wait_send()
+    for store in stores:
+        store.wait()
     halo_done(0, 0, 0)
+    halo_done(0, 0, 1)
     for s in range(1, 4):
         for t in range(2):
             for c in range(3):
@@ -538,17 +550,17 @@
     wide = (3 * ROWS, 2 * LANES)
     vmem = pl.BlockSpec(memory_space=pltpu.VMEM)
     smem = pl.BlockSpec(memory_space=pltpu.SMEM)
-    place = pl.BlockSpec(memory_space=pl.ANY)
+    hbm = pl.BlockSpec(memory_space=pltpu.HBM)
     dma = pltpu.SemaphoreType.DMA
     grads = pl.pallas_call(
         functools.partial(kernel, rows_n, length),
         out_shape=jax.ShapeDtypeStruct((2, ROWS, 2, 2 * LANES), F32),
-        in_specs=[smem, smem, vmem, place, place],
-        out_specs=vmem,
+        in_specs=[smem, smem, vmem, hbm, hbm],
+        out_specs=pl.BlockSpec(memory_space=pl.ANY),
         scratch_shapes=[
             pltpu.VMEM((2, ROWS, 2, 2 * LANES), BF16),
             pltpu.VMEM((ROWS, 2, 2 * LANES), F32),
-            pltpu.VMEM((2, 3, ROWS, 2, PIECE), BF16),
+            pltpu.VMEM((2, ROWS, 2, UNITS * LANES), BF16),
             pltpu.VMEM((ROWS, 2, PIECE), F32),
             pltpu.VMEM((UNITS,) + wide, BF16),
             pltpu.VMEM((UNITS,) + unit, BF16),
@@ -571,7 +583,8 @@
             pltpu.VMEM((UNITS,) + unit, BF16),
             pltpu.VMEM((3, 2) + unit, BF16),
             pltpu.VMEM((3, 2) + unit, BF16),
-            dma((1 + UNITS,)),
+            pltpu.VMEM((2, ROWS, 2, 2 * LANES), F32),
+            dma((4,)),
             dma((2, 3)),
             dma((2, 3)),
             dma((2, 3)),
@@ -580,15 +593,23 @@
             dma((2,)),
             dma,
             dma,
-            dma((UNITS,)),
-            dma((UNITS,)),
+            dma((3,)),
+            dma((3,)),
             dma((4, 2, 3, 2)),
             dma((4, 2, 3, 2)),
             dma((2, 3)),
             dma((2, 3)),
         ],
-        compiler_params=pltpu.CompilerParams(collective_id=0, has_side_effects=True),
-    )(chosen, angle_freq.T, kernel_taps, slices, measured)
+        compiler_params=pltpu.CompilerParams(
+            collective_id=0, has_side_effects=True, vmem_limit_bytes=24 * 2**20
+        ),
+    )(
+        chosen,
+        angle_freq.T,
+        kernel_taps,
+        pltpu.with_memory_space_constraint(slices, pltpu.HBM),
+        pltpu.with_memory_space_constraint(measured, pltpu.HBM),
+    )
     return grads[0], grads[1]
 
 

time: 61.9 us -> 60.3 us (0.974)
  Pallas kernels: 58.8 us -> 57.5 us
    pallas_call x1, Pallas kernels: 58.8 us -> 57.5 us  [local(): pl.pallas_call(functools.partial(kernel, rows_n, length), out_shape=jax.S...]
    squeeze x1, local copies, waits for them, and re-layouts: 1.53 us -> 0.66 us  [local(): return (grads[0], grads[1])]
    unnamed x0 -> x4, local copies, waits for them, and re-layouts: none -> 0.67 us
where the time goes in v4:
time: 60.3 us; the launch traced here: 60.2 us
  Pallas kernels  57.5 us (95%)
  local copies, waits for them, and re-layouts  1.33 us (2%)
  between operations  1.3 us (2%)
    pallas_call x1, Pallas kernels, local(): pl.pallas_call(functools.partial(kernel, rows_n, length), out_shape=jax.S...  57.5 us

profile of v4, /device:TPU:224, one launch (start us, length us, event | category | flops | bytes accessed | tf_op | source)
XLA Modules:
  0.0 60.2 jit_solution(11458956115970780472)
XLA Ops:
  1.3 0.0 copy-start
  1.3 0.0 copy-start.1
  1.3 0.7 %copy-done = f32[128,2]{0,1:T(2,128)S(1)} copy-done((f32[128,2]{0,1:T(2,128)S(1)}, f32[128,2]{0,1:T(2,128)}, u32[]{:S(2)}) %copy-start) | copy-done | bytes 1048
  2.0 0.0 copy-done.1
  2.0 57.5 %shard_map.68 = f32[2,32,2,256]{3,2,1,0:T(2,128)S(1)} custom-call(s32[1]{0:T(128)S(6)} %copy.7.chosen_ref, f32[2,128]{1,0:T(2,128)S(1)} %bitcast.5, bf16[2,65]{1,0:T(2,128)(2,1)S(1)} %copy-done.1, bf16[2,32,2,256]{3,2,1,0:T(2,128)(2,1)} %slices_ref.1, bf16[1,32,2,2048]{3,2,1,0:T(2,128)(2,1)} %meas_ref.1), custom_call_target="tpu_custom_call" | custom-call | tf_op jit(solution)/shard_map/pallas_call | solution.py:555
  59.5 0.7 %slice_bitcast_fusion = (f32[32,2,256]{2,1,0:T(2,128)}, f32[32,2,256]{2,1,0:T(2,128)}) fusion(f32[2,32,2,256]{3,2,1,0:T(2,128)S(1)} %shard_map.68), kind=kLoop, calls=%fused_computation | loop fusion | bytes 262144 | tf_op jit(solution)/shard_map/squeeze | solution.py:613
Async XLA Ops:
  1.3 0.7 %copy-start = (f32[128,2]{0,1:T(2,128)S(1)}, f32[128,2]{0,1:T(2,128)}, u32[]{:S(2)}) copy-start(f32[128,2]{0,1:T(2,128)} %param.8) | copy-start | bytes 3076
  1.3 0.7 %copy-start.1 = (bf16[2,65]{1,0:T(2,128)(2,1)S(1)}, bf16[2,65]{1,0:T(2,128)(2,1)}, u32[]{:S(2)}) copy-start(bf16[2,65]{1,0:T(2,128)(2,1)} %taps_ref.1) | copy-start | bytes 784

commit v5 on v4

--- a/solution.py
+++ b/solution.py
@@ -490,13 +490,13 @@
     for k in range(1, 4):
         slab_wait(1, k)
     enter(0)
+    margin_wait(1)
+    second(0)
     freq_copy.wait_recv()
     waves(1, other_freq)
     enter(1)
+    second(1)
     meas_load.wait()
-    margin_wait(1)
-    second(0)
-    second(1)
     for c in range(3):
         compare(0, c)
     for c in range(3):
@@ -605,8 +605,8 @@
         ),
     )(
         chosen,
-        angle_freq.T,
-        kernel_taps,
+        pltpu.with_memory_space_constraint(angle_freq.T, pltpu.HBM),
+        pltpu.with_memory_space_constraint(kernel_taps, pltpu.HBM),
         pltpu.with_memory_space_constraint(slices, pltpu.HBM),
         pltpu.with_memory_space_constraint(measured, pltpu.HBM),
     )

time: 60.3 us -> 59 us (0.978)
  local copies, waits for them, and re-layouts: 1.33 us -> 0.66 us
    unnamed x4 -> x0, local copies, waits for them, and re-layouts: 0.67 us -> none
    pallas_call x1, Pallas kernels: 57.5 us -> 56.9 us  [local(): pl.pallas_call(functools.partial(kernel, rows_n, length), out_shape=jax.S...]
where the time goes in v5:
time: 59 us; the launch traced here: 58.8 us
  Pallas kernels  56.9 us (96%)
  between operations  1.29 us (2%)
  local copies, waits for them, and re-layouts  0.66 us (1%)
    pallas_call x1, Pallas kernels, local(): pl.pallas_call(functools.partial(kernel, rows_n, length), out_shape=jax.S...  56.9 us

profile of v5, /device:TPU:224, one launch (start us, length us, event | category | flops | bytes accessed | tf_op | source)
XLA Modules:
  0.0 58.8 jit_solution(11052744010220733559)
XLA Ops:
  1.3 56.9 %shard_map.68 = f32[2,32,2,256]{3,2,1,0:T(2,128)S(1)} custom-call(s32[1]{0:T(128)S(6)} %copy.7.chosen_ref, f32[2,128]{1,0:T(2,128)} %bitcast.5, bf16[2,65]{1,0:T(2,128)(2,1)} %taps_ref.1, bf16[2,32,2,256]{3,2,1,0:T(2,128)(2,1)} %slices_ref.1, bf16[1,32,2,2048]{3,2,1,0:T(2,128)(2,1)} %meas_ref.1), custom_call_target="tpu_custom_call" | custom-call | tf_op jit(solution)/shard_map/pallas_call | solution.py:555
  58.2 0.7 %slice_bitcast_fusion = (f32[32,2,256]{2,1,0:T(2,128)}, f32[32,2,256]{2,1,0:T(2,128)}) fusion(f32[2,32,2,256]{3,2,1,0:T(2,128)S(1)} %shard_map.68), kind=kLoop, calls=%fused_computation | loop fusion | bytes 262144 | tf_op jit(solution)/shard_map/squeeze | solution.py:613

commit v6 on v5

--- a/solution.py
+++ b/solution.py
@@ -374,13 +374,16 @@
             first[t, u0:u1] = columns(entry.at[t], wf, u0, u1)
 
     def second(t):
-        for u in range(UNITS):
-            re, im = row_correlate(rf, first[t, u])
-            value = join(re, im).astype(BF16)
-            inner[t, u] = value
-            re, im = times(*parts(far[u]), *parts(value))
-            field[t, u + 1] = join(re, im).astype(BF16)
+        at = 0
         for c, (u0, u1) in enumerate(PARTS):
+            ahead = min(u1 + 1, UNITS)
+            for u in range(at, ahead):
+                re, im = row_correlate(rf, first[t, u])
+                value = join(re, im).astype(BF16)
+                inner[t, u] = value
+                re, im = times(*parts(far[u]), *parts(value))
+                field[t, u + 1] = join(re, im).astype(BF16)
+            at = ahead
             own(1, t, u0, u1, columns(field.at[t], wf, u0, u1))
             halo_start(1, t, c)
 

time: 59 us -> 59 us (level)
  no operation moved by 1% of the time
where the time goes in v6:
time: 59 us; the launch traced here: 58.9 us
  Pallas kernels  56.9 us (96%)
  between operations  1.29 us (2%)
  local copies, waits for them, and re-layouts  0.66 us (1%)
    pallas_call x1, Pallas kernels, local(): pl.pallas_call(functools.partial(kernel, rows_n, length), out_shape=jax.S...  56.9 us

profile of v6, /device:TPU:224, one launch (start us, length us, event | category | flops | bytes accessed | tf_op | source)
XLA Modules:
  0.0 58.9 jit_solution(16875509721671564329)
XLA Ops:
  1.3 56.9 %shard_map.68 = f32[2,32,2,256]{3,2,1,0:T(2,128)S(1)} custom-call(s32[1]{0:T(128)S(6)} %copy.7.chosen_ref, f32[2,128]{1,0:T(2,128)} %bitcast.5, bf16[2,65]{1,0:T(2,128)(2,1)} %taps_ref.1, bf16[2,32,2,256]{3,2,1,0:T(2,128)(2,1)} %slices_ref.1, bf16[1,32,2,2048]{3,2,1,0:T(2,128)(2,1)} %meas_ref.1), custom_call_target="tpu_custom_call" | custom-call | tf_op jit(solution)/shard_map/pallas_call | solution.py:558
  58.2 0.7 %slice_bitcast_fusion = (f32[32,2,256]{2,1,0:T(2,128)}, f32[32,2,256]{2,1,0:T(2,128)}) fusion(f32[2,32,2,256]{3,2,1,0:T(2,128)S(1)} %shard_map.68), kind=kLoop, calls=%fused_computation | loop fusion | bytes 262144 | tf_op jit(solution)/shard_map/squeeze | solution.py:616
